TPU v7x, 32 devices: a whole 2x2x4 slice. The times are simulated.
32 devices in a mesh: batch: 8 (over z, core), vocab: 4 (over y, x).
Axes of the slice: x: 2, y: 2, z: 4, core: 2. Of those that a mesh axis runs over, the one named last changes fastest.
Arguments:
- hidden: bfloat16 [1024, 4096], P('batch'), may hold values from -40 to 40
- exit_layer: int32 [1024], P('batch'), may hold values from 0 to 7
- exit_gains: float32 [8, 4096], replicated, may hold values from 0.1 to 1.9
- unembed: bfloat16 [4096, 128256], P(None, ('batch', 'vocab')), may hold values from -10 to 10
- targets: int32 [1024], replicated, may hold values from 0 to 128255
- values: float32 [1024], P('batch'), may hold values from -6 to 6
- rewards: float32 [1024], P('batch'), may hold values from -2 to 2
- ref_logprob: float32 [1024], P('batch'), may hold values from -16 to -6
- segment_end: int32 [1024], P('batch'), may hold values 0 or 1
Outputs:
- logprob: float32 [1024], P('batch')
- advantages: float32 [1024], P('batch')
All inputs are finite; a program needn't handle non-finite values. No bound on the sum of `segment_end` on one device may be relied on, other than what follows from the above.
Results may differ from a plain program's by a relative error of at most 0.00054.
Values may be sent and summed in bfloat16 or wider, within the bound.
No kernel may reach another device: no remote copies, remote signals or barrier semaphores. Data moves between devices by JAX's collectives and lax.ppermute only.
A program may use at most 128 MiB of HBM per device.

v0:
```python
import jax
import jax.numpy as jnp
from jax import lax
from jax.sharding import PartitionSpec as P

epsilon_norm = 1e-05
discount = 1.0
trace_decay = 0.999
penalty_weight = 0.1


def joined(part, axis, combine):
    gathered = jax.tree.map(lambda a: lax.all_gather(a, axis), part)

    def take(source):
        return jax.tree.map(lambda a: lax.dynamic_index_in_dim(a, source, 0, False), gathered)

    return lax.fori_loop(
        1, lax.axis_size(axis), lambda source, state: combine(state, take(source)), take(0)
    )


def from_behind(value, axis, steps):
    count = lax.axis_size(axis)
    initial, last = (max(0, -steps), min(count, count - steps))
    return lax.ppermute(value, axis, [(source, source + steps) for source in range(initial, last)])


def normalize(rows, layers, exit_gains):
    states = rows.astype(jnp.float32)
    inverse = lax.rsqrt(jnp.mean(states * states, axis=-1, keepdims=True) + epsilon_norm)
    selector = (
        layers[:, None] == jnp.arange(exit_gains.shape[0], dtype=jnp.int32)[None, :]
    ).astype(jnp.float32)
    scaling = jnp.dot(selector, exit_gains, precision=lax.Precision.HIGHEST)
    return (states * inverse * scaling).astype(jnp.bfloat16)


def per_device(
    hidden, exit_layer, exit_gains, unembed, targets, values, rewards, ref_logprob, segment_end
):
    column_count = unembed.shape[1]
    column_start = lax.axis_index(("batch", "vocab")) * column_count
    columns = jnp.arange(column_count, dtype=jnp.int32)
    total_rows = targets.shape[0]
    owned = hidden.shape[0]
    peers = lax.axis_size("batch")
    width = hidden.shape[1]
    normed = normalize(hidden, exit_layer, exit_gains)
    gathered = lax.all_gather(normed, "batch", axis=0, tiled=True)
    block_rows = 512
    block_count = total_rows // block_rows

    def score_block(pair):
        rows_block, ids_block = pair
        logits = jnp.dot(rows_block, unembed, preferred_element_type=jnp.float32)
        row_max = jnp.max(logits, axis=1)
        row_total = jnp.sum(jnp.exp(logits - row_max[:, None]), axis=1)
        wanted = ids_block - column_start
        picked = jnp.sum(jnp.where(columns[None, :] == wanted[:, None], logits, 0.0), axis=1)
        return (row_max, row_total, picked)

    maxima, totals, picks = lax.map(
        score_block,
        (
            gathered.reshape(block_count, block_rows, width),
            targets.reshape(block_count, block_rows),
        ),
    )
    maxima = maxima.reshape(total_rows)
    totals = totals.reshape(total_rows)
    picks = picks.reshape(total_rows)
    maxima, totals, picks = (
        lax.all_to_all(maxima, "batch", split_axis=0, concat_axis=0, tiled=True),
        lax.all_to_all(totals, "batch", split_axis=0, concat_axis=0, tiled=True),
        lax.all_to_all(picks, "batch", split_axis=0, concat_axis=0, tiled=True),
    )
    maxima = maxima.reshape(peers, owned)
    totals = totals.reshape(peers, owned)
    picks = picks.reshape(peers, owned)
    group_max = jnp.max(maxima, axis=0)
    group_total = jnp.sum(totals * jnp.exp(maxima - group_max[None, :]), axis=0)
    group_pick = jnp.sum(picks, axis=0)

    def combine_groups(first, second):
        larger = jnp.maximum(first[0], second[0])
        summed = first[1] * jnp.exp(first[0] - larger) + second[1] * jnp.exp(second[0] - larger)
        return (larger, summed, first[2] + second[2])

    overall_max, overall_total, overall_pick = joined(
        (group_max, group_total, group_pick), "vocab", combine_groups
    )
    logprob = overall_pick - (overall_max + jnp.log(overall_total))
    following = from_behind(values[:1], "batch", -1)
    next_values = jnp.concatenate([values[1:], following])
    keeping = 1.0 - segment_end.astype(jnp.float32)
    shaped = rewards - penalty_weight * (logprob - ref_logprob)
    deltas = shaped + discount * next_values * keeping - values
    factors = discount * trace_decay * keeping

    def backward(running, inputs):
        factor, delta = inputs
        accrued = delta + factor * running[0]
        product = factor * running[1]
        return ((accrued, product), (accrued, product))

    finished, outputs = lax.scan(
        backward,
        (jnp.zeros((), jnp.float32), jnp.ones((), jnp.float32)),
        (factors, deltas),
        reverse=True,
    )
    local_adv, products = outputs
    head_adv = local_adv[:1]
    head_prod = products[:1]

    def relay_step(index, inbound):
        return from_behind(head_adv + head_prod * inbound, "batch", -1)

    incoming = lax.fori_loop(0, peers - 1, relay_step, jnp.zeros((1,), jnp.float32))
    advantages = local_adv + products * incoming
    return (logprob, advantages)


def solution(mesh):
    placed = (
        P("batch", None),
        P("batch"),
        P(),
        P(None, ("batch", "vocab")),
        P(),
        P("batch"),
        P("batch"),
        P("batch"),
        P("batch"),
    )
    return jax.shard_map(
        per_device, mesh=mesh, in_specs=placed, out_specs=(P("batch"), P("batch")), check_vma=False
    )
```

profile of v0, /device:TPU:1, one launch (start us, length us, event | category | flops | bytes accessed | tf_op | source)
XLA Modules:
  0.0 659.9 jit_solution(1969965212118673331)
XLA Ops:
  8.8 3.4 fusion.13
  12.9 83.9 %all-gather.8.cloned.1.call-done = bf16[1024,4096]{1,0:T(8,128)(2,1)} async-done(((bf16[128,4096]{1,0:T(8,128)(2,1)}), bf16[1024,4096]{1,0:T(8,128)(2,1)}) %all-gather.8.cloned.1.call-update) | async-done | bytes 8388624 | tf_op jit(solution)/shard_map/all_gather | solution.py:50
  96.8 49.9 %while.67 = (s32[]{:T(128)}, f32[2,512]{1,0:T(2,128)S(1)}, f32[2,512]{1,0:T(2,128)S(1)}, f32[2,512]{1,0:T(2,128)S(1)}, bf16[2,512,4096]{2,1,0:T(8,128)(2,1)}, /*...) while((s32[]{:T(128)}, f32[2,512]{1,0:T(2,128)S(1)}, ...), condition=%wide.region_5.6_spmd.clone, body=%wide.region_1.5_spmd.clone.sunk | while | flops 16823081984 | bytes 53471864 | solution.py:63
  96.9 22.6 %fusion.28 = (f32[512]{0:T(512)S(1)}, f32[512,4008]{0,1:T(8,128)S(1)}) fusion(bf16[4096,4008]{0,1:T(8,128)(2,1)} %get-tuple-element.681, bf16[2,512,4096]{2,1,0:T(8,128)(2,1)} %get-tuple-element.680, s32[]{:T(128)} %get-tuple-element.666), kind=kOutput, calls=%fused_computation.38.clone.1 | convolution fusion | flops 16812822528 | bytes 45238784 | tf_op jit(solution)/shard_map/while/body/eval_jaxpr/dot_general | solution.py:56
  119.5 2.2 select_reduce_fusion.2
  121.8 22.6 %fusion.28 = (f32[512]{0:T(512)S(1)}, f32[512,4008]{0,1:T(8,128)S(1)}) fusion(bf16[4096,4008]{0,1:T(8,128)(2,1)} %get-tuple-element.681, bf16[2,512,4096]{2,1,0:T(8,128)(2,1)} %get-tuple-element.680, s32[]{:T(128)} %get-tuple-element.666), kind=kOutput, calls=%fused_computation.38.clone.1 | convolution fusion | flops 16812822528 | bytes 45238784 | tf_op jit(solution)/shard_map/while/body/eval_jaxpr/dot_general | solution.py:56
  144.4 2.2 select_reduce_fusion.2
  147.3 3.4 all-to-all-start
  151.4 4.3 all-to-all-done
  155.7 3.9 all-to-all-start.1
  159.6 2.0 collective-permute-start.1
  162.3 2.2 all-to-all-done.1
  164.5 3.9 all-to-all-start.2
  168.4 5.9 all-gather.4
  174.3 5.9 all-gather.5
  180.2 5.0 all-gather.3
  186.4 421.8 %while.65 = (s32[]{:T(128)}, f32[]{:T(128)}, f32[]{:T(128)}, f32[128]{0:T(128)S(1)}, f32[128]{0:T(128)S(1)}, /*index=5*/f32[128]{0:T(128)S(1)}, f32[128]{0:T(128)S(1)}, s32[]{:T(128)}, s32[]{:T(128)}) while((s32[]{:T(128)}, f32[]{:T(128)}, f32[]{:T(128)}, f32[128]{0:T(128)S(1)}, f32[128]{0:T(128)S(1)}, /*index=5*/f32[128]{0:T(128)S(1)}, ...), condition=%wide.region_12.13_spmd, body=%wide.region_11.12_spmd.sunk | while | flops 6 | bytes 189 | solution.py:107
  608.2 44.3 %while.66 = (s32[]{:T(128)}, f32[1]{0:T(128)}, f32[1]{0:T(128)S(1)}, f32[1]{0:T(128)S(1)}, s32[]{:T(128)}) while((s32[]{:T(128)}, f32[1]{0:T(128)}, f32[1]{0:T(128)S(1)}, f32[1]{0:T(128)S(1)}, s32[]{:T(128)}) %tuple.128), condition=%wide.region_14.15_spmd, body=%wide.region_13.14_spmd.sunk | while | flops 4 | bytes 141 | solution.py:120
  608.3 9.0 %collective-permute-start = (f32[1]{0:T(128)}, f32[1]{0:T(128)}, u32[]{:S(2)}, u32[]{:S(2)}) collective-permute-start(f32[1]{0:T(128)} %add.147), channel_id=1, source_target_pairs={{4,0},{8,4},{12,8},{16,12},{20,16},{24,20},{28,24},{5,1},{9,5},{13... | collective-permute-start | bytes 20 | tf_op jit(solution)/shard_map/while/body/eval_jaxpr/ppermute | solution.py:26
  617.3 1.8 collective-permute-done
  619.8 2.9 collective-permute-start
  622.6 2.0 collective-permute-done
  625.2 2.9 collective-permute-start
  628.1 2.0 collective-permute-done
  630.7 2.9 collective-permute-start
  633.6 2.0 collective-permute-done
  636.2 2.9 collective-permute-start
  639.1 2.0 collective-permute-done
  641.7 2.9 collective-permute-start
  644.5 2.0 collective-permute-done
  647.2 2.9 collective-permute-start
  650.0 2.0 collective-permute-done
  (558 shorter events, 190.8 us)
Async XLA Ops:
  7.2 1.6 copy-start
  7.2 89.7 %all-gather.8.cloned.1.call-start = ((), (), s32[]{:S(2)}) async-start(), calls=%async_computation.3 | async-start | bytes 9437184 | tf_op jit(solution)/shard_map/all_gather | solution.py:50
  96.8 62.7 %copy-start.1 = (f32[128]{0:T(128)S(1)}, f32[128]{0:T(128)}, u32[]{:S(2)}) copy-start(f32[128]{0:T(128)} %param.22) | copy-start | bytes 1540
  96.8 88.4 %copy-start.2 = (f32[128]{0:T(128)S(1)}, f32[128]{0:T(128)}, u32[]{:S(2)}) copy-start(f32[128]{0:T(128)} %param.23) | copy-start | bytes 1540
  96.8 88.4 %copy-start.3 = (f32[128]{0:T(128)S(1)}, f32[128]{0:T(128)}, u32[]{:S(2)}) copy-start(f32[128]{0:T(128)} %param.24) | copy-start | bytes 1540
  96.8 88.4 %copy-start.4 = (s32[128]{0:T(128)S(1)}, s32[128]{0:T(128)}, u32[]{:S(2)}) copy-start(s32[128]{0:T(128)} %param.25) | copy-start | bytes 1540
  147.3 8.4 %all-to-all-start = ((f32[8,128,1]{1,2,0:T(1,128)}), f32[8,128,1]{1,2,0:T(1,128)S(1)}, u32[]{:S(2)}, u32[]{:S(2)}) async-start(f32[8,128,1]{1,2,0:T(1,128)} %all_to_all.18), calls=%async_computation | async-start | bytes 8192 | tf_op jit(solution)/shard_map/all_to_all | solution.py:74
  155.7 8.8 %all-to-all-start.1 = ((f32[8,128,1]{1,2,0:T(1,128)}), f32[8,128,1]{1,2,0:T(1,128)S(1)}, u32[]{:S(2)}, u32[]{:S(2)}) async-start(f32[8,128,1]{1,2,0:T(1,128)} %all_to_all.20), calls=%async_computation.1 | async-start | bytes 8192 | tf_op jit(solution)/shard_map/all_to_all | solution.py:75
  159.6 25.7 %collective-permute-start.1 = (f32[1]{0:T(128)S(1)}, f32[1]{0:T(128)}, u32[]{:S(2)}, u32[]{:S(2)}) collective-permute-start(f32[1]{0:T(128)S(1)} %bitcast.85), channel_id=1, source_target_pairs={{4,0},{8,4},{12,8},{16,12},{20,16},{24,20},{28,24},{5,1},{9,5},{13... | collective-permute-start | bytes 20 | tf_op jit(solution)/shard_map/ppermute | solution.py:26
  164.5 9.8 %all-to-all-start.2 = ((f32[8,128,1]{1,2,0:T(1,128)}), f32[8,128,1]{1,2,0:T(1,128)S(1)}, u32[]{:S(2)}, u32[]{:S(2)}) async-start(f32[8,128,1]{1,2,0:T(1,128)} %all_to_all.22), calls=%async_computation.2 | async-start | bytes 8192 | tf_op jit(solution)/shard_map/all_to_all | solution.py:76
  608.3 10.8 %collective-permute-start = (f32[1]{0:T(128)}, f32[1]{0:T(128)}, u32[]{:S(2)}, u32[]{:S(2)}) collective-permute-start(f32[1]{0:T(128)} %add.147), channel_id=1, source_target_pairs={{4,0},{8,4},{12,8},{16,12},{20,16},{24,20},{28,24},{5,1},{9,5},{13... | collective-permute-start | bytes 20 | tf_op jit(solution)/shard_map/while/body/eval_jaxpr/ppermute | solution.py:26
  619.8 4.8 collective-permute-start
  625.2 4.8 collective-permute-start
  630.7 4.8 collective-permute-start
  636.2 4.8 collective-permute-start
  641.7 4.8 collective-permute-start
  647.2 4.8 collective-permute-start
Sparse Core Ops, SparseCore 0:
  12.3 84.4 all-gather.7
where the time goes:
time: 664 us; the launch traced here: 660 us
  loops' own time  242 us (36%)
  local copies, waits for them, and re-layouts  187 us (28%)
  waiting for transfers between devices  104 us (16%)
  matrix products  48.5 us (7%)
  starting transfers between devices  39.4 us (6%)
  blocking collectives  16.7 us (3%)
  between operations  14.1 us (2%)
  other arithmetic  7.76 us (1%)
    another operation x1, loops' own time, per_device(): lax.scan(backward, (jnp.zeros((), jnp.float32), jnp.ones((), jnp.float32)...  237 us
    dynamic_slice x256, local copies, waits for them, and re-layouts, per_device(): lax.scan(backward, (jnp.zeros((), jnp.float32), jnp.ones((), jnp.float32)...  155 us
    all_gather x1, waiting for transfers between devices, per_device(): gathered = lax.all_gather(normed, 'batch', axis=0, tiled=True)  83.9 us
    dot_general x2, matrix products, score_block(): logits = jnp.dot(rows_block, unembed, preferred_element_type=jnp.float32)  45.2 us
    dynamic_update_slice x256, local copies, waits for them, and re-layouts, per_device(): lax.scan(backward, (jnp.zeros((), jnp.float32), jnp.ones((), jnp.float32)...  29.4 us
    ppermute x8, starting transfers between devices, from_behind(): lax.ppermute(value, axis, [(source, source + steps) for source in range(i...  28.2 us
    all_gather x3, blocking collectives, joined(): gathered = jax.tree.map(lambda a: lax.all_gather(a, axis), part)  16.7 us
    ppermute x8, waiting for transfers between devices, from_behind(): lax.ppermute(value, axis, [(source, source + steps) for source in range(i...  13.7 us
  transfers between devices with their start and end apart: 12, of which 10 were waited for; matrix products, arithmetic and copies ran while one was open for 0% of the time, Pallas kernels for 0%

commit v1 on v0

v1 whole, which is shorter than its diff:
```python
import math

import jax
import jax.numpy as jnp
from jax import lax
from jax.experimental import pallas as pl
from jax.experimental.pallas import tpu as pltpu
from jax.sharding import PartitionSpec as P

epsilon_norm = 1e-05
discount = 1.0
trace_decay = 0.999
penalty_weight = 0.1
CORES = 2
LOWEST = float(jnp.finfo(jnp.float32).min)
VMEM = pl.BlockSpec(memory_space=pltpu.VMEM)
ANY = pl.BlockSpec(memory_space=pl.ANY)
HBM = pl.BlockSpec(memory_space=pltpu.HBM)
RESIDENT = True
MIB = 2**20


class Grid:
    def __init__(self, mesh):
        self.peers, self.groups = mesh.shape["batch"], mesh.shape["vocab"]
        self.planes = self.peers // CORES
        self.side = math.isqrt(self.groups)

    def moves(self, target):
        pairs = []
        for b in range(self.peers):
            for v in range(self.groups):
                z, c, y, x = target(b // CORES, b % CORES, v // self.side, v % self.side)
                pairs.append((b * self.groups + v, (z * CORES + c) * self.groups + y * self.side + x))
        return pairs

    def send(self, array, target):
        return lax.ppermute(array, ("batch", "vocab"), self.moves(target))

    def twin(self, array):
        return self.send(array, lambda z, c, y, x: (z, 1 - c, y, x))

    def up(self, array):
        return self.send(array, lambda z, c, y, x: ((z + 1) % self.planes, c, y, x))

    def along_x(self, array):
        return self.send(array, lambda z, c, y, x: (z, c, y, x ^ 1))

    def along_y(self, array):
        return self.send(array, lambda z, c, y, x: (z, c, y ^ 1, x))

    def place(self):
        b, v = lax.axis_index("batch"), lax.axis_index("vocab")
        half = lax.rem(lax.div(v, self.side) + lax.rem(v, self.side), 2)
        return lax.div(b, CORES), lax.rem(b, CORES), half


def normalize_kernel(grid, hidden_ref, layers_ref, gains_ref, out_ref, half_ref):
    rows = hidden_ref.shape[0]
    block = 16
    exits = gains_ref.shape[0]
    layers = jnp.broadcast_to(layers_ref[...], (rows, rows)).astype(jnp.float32).T
    for begin in range(0, rows, block):
        part = pl.ds(begin, block)
        states = hidden_ref[part, :].astype(jnp.float32)
        mean = jnp.sum(states * states, axis=1, keepdims=True) / states.shape[1]
        inverse = lax.rsqrt(mean + epsilon_norm)
        layer = layers[begin : begin + block, :1]
        scaling = jnp.broadcast_to(gains_ref[0:1, :], states.shape)
        for index in range(1, exits):
            scaling = jnp.where(layer == float(index), gains_ref[index : index + 1, :], scaling)
        out_ref[part, :] = (states * inverse * scaling).astype(out_ref.dtype)
    half = grid.place()[2]
    length = rows // 2
    half_ref[...] = out_ref[pl.ds(pl.multiple_of(half * length, length), length), :]


def spans(rows, target):
    count = max(1, round(rows / target))
    size = -(-rows // (count * 16)) * 16
    return [(begin, min(size, rows - begin)) for begin in range(0, rows, size)]


def tally(logits, begin, wanted, carry):
    old, total, pick = carry
    place = lax.broadcasted_iota(jnp.int32, logits.shape, 0) + begin
    new = jnp.maximum(old, jnp.max(logits, axis=0, keepdims=True))
    total = total * jnp.exp(old - new) + jnp.sum(jnp.exp(logits - new), axis=0, keepdims=True)
    pick = pick + jnp.sum(jnp.where(place == wanted, logits, 0.0), axis=0, keepdims=True)
    return new, total, pick


def product(weights, states):
    return lax.dot_general(
        weights, states, (((1,), (1,)), ((), ())), preferred_element_type=jnp.float32
    )


def score_kernel(grid, step, pieces, first, last, *refs):
    refs = list(refs)
    ids_ref, weights_in = refs.pop(0), refs.pop(0)
    parts_in = None if first else refs.pop(0)
    values_ref = refs.pop(0) if last else None
    piece_refs = [refs.pop(0) for _ in pieces]
    parts_ref = refs.pop(0)
    weights_ref = weights_in
    states_ref, piece_sem = refs.pop(0), refs.pop(0)
    rows = weights_ref.shape[0]
    plane, core, half = grid.place()
    source = lax.rem(plane - step + grid.planes, grid.planes)
    copies = []
    for index, (piece, ref) in enumerate(zip(pieces, piece_refs)):
        offset = pl.multiple_of(piece(core, half), ref.shape[0])
        copies.append(
            pltpu.make_async_copy(ref, states_ref.at[pl.ds(offset, ref.shape[0])], piece_sem.at[index])
        )
    for copy in copies:
        copy.start()
    blocks = spans(rows, 1336)
    fetches = []
    for copy in copies:
        copy.wait()
    start = (lax.axis_index("batch") * grid.groups + lax.axis_index("vocab")) * rows
    wanted = ids_ref[source] - start
    tokens = states_ref.shape[0]
    carry = (
        jnp.full((1, tokens), LOWEST, jnp.float32),
        jnp.zeros((1, tokens), jnp.float32),
        jnp.zeros((1, tokens), jnp.float32),
    )
    pending = None
    for index, (begin, size) in enumerate(blocks):
        logits = product(weights_ref[begin : begin + size, :], states_ref[...])
        if pending is not None:
            carry = tally(*pending, wanted, carry)
        pending = (logits, begin)
    carry = tally(*pending, wanted, carry)
    owned = tokens // CORES
    if not last:
        if not first:
            parts_ref[...] = parts_in[...]
        for index in range(3):
            parts_ref[source, index : index + 1, :] = carry[index]
        return
    for group in range(grid.planes):
        here = source == group
        for index in range(4):
            if index < 3:
                row = jnp.where(here, carry[index], parts_in[group, index : index + 1, :])
            else:
                row = jnp.broadcast_to(values_ref[0:1, 0:1], (1, tokens))
            for side in range(CORES):
                part = row[:, side * owned : (side + 1) * owned]
                for column in range(grid.groups):
                    parts_ref[(group * CORES + side) * grid.groups + column, index : index + 1, :] = part


def score(grid, step, pieces, ids, weights, parts, values, first, last):
    owned = pieces[0][1].shape[0] if first else pieces[0][1].shape[0] * 2
    width = weights.shape[1]
    rows = weights.shape[0]
    tokens = owned * CORES
    if last:
        out_shape = jax.ShapeDtypeStruct((grid.peers * grid.groups, 4, owned), jnp.float32)
    else:
        out_shape = jax.ShapeDtypeStruct((grid.planes, 3, tokens), jnp.float32)
    args = [ids, weights]
    specs = [VMEM, VMEM]
    if not first:
        args.append(parts)
        specs.append(VMEM)
    if last:
        args.append(values)
        specs.append(VMEM)
    args += [array for _, array in pieces]
    specs += [HBM] * len(pieces)
    scratch = [
        pltpu.VMEM((tokens, width), jnp.bfloat16),
        pltpu.SemaphoreType.DMA((len(pieces),)),
    ]
    out_specs = VMEM
    limit = 8
    offsets = [offset for offset, _ in pieces]
    return pl.pallas_call(
        lambda *refs: score_kernel(grid, step, offsets, first, last, *refs),
        out_shape=out_shape,
        in_specs=specs,
        out_specs=out_specs,
        scratch_shapes=scratch,
        compiler_params=pltpu.CompilerParams(vmem_limit_bytes=limit * MIB),
        cost_estimate=pl.CostEstimate(
            flops=2 * rows * tokens * width, transcendentals=rows * tokens, bytes_accessed=0
        ),
        name=f"score{step}",
    )(*args)


def load_kernel(weights_in, weights_ref, sem):
    copy = pltpu.make_async_copy(weights_in, weights_ref, sem)
    copy.start()
    copy.wait()


def tail_kernel(grid, parts_ref, values_ref, rewards_ref, anchor_ref, ends_ref,
                logprob_ref, heads_ref, accrued_ref, product_ref):
    here = lax.axis_index("batch")
    peers = grid.peers
    owned = values_ref.shape[1]
    maxima = parts_ref[:, 0, :]
    larger = jnp.max(maxima, axis=0, keepdims=True)
    total = jnp.sum(parts_ref[:, 1, :] * jnp.exp(maxima - larger), axis=0, keepdims=True)
    picked = jnp.sum(parts_ref[:, 2, :], axis=0, keepdims=True)
    logprob = picked - (larger + jnp.log(total))
    logprob_ref[...] = logprob
    place = lax.broadcasted_iota(jnp.int32, (8, owned), 1)

    def wide(row):
        return jnp.broadcast_to(row, (8, owned))

    def ahead(array, steps):
        return pltpu.roll(array, owned - steps, 1)

    behind = jnp.minimum(here + 1, peers - 1)
    entering = wide(parts_ref[pl.ds(behind * grid.groups, 1), 3, :])
    entering = jnp.where(here + 1 < peers, entering, 0.0)
    values = wide(values_ref[...])
    following = jnp.where(place < owned - 1, ahead(values, 1), entering)
    keeping = 1.0 - wide(ends_ref[...]).astype(jnp.float32)
    shaped = wide(rewards_ref[...]) - penalty_weight * (wide(logprob) - wide(anchor_ref[...]))
    accrued = shaped + discount * following * keeping - values
    product = discount * trace_decay * keeping
    steps = 1
    while steps < owned:
        inside = place < owned - steps
        accrued = accrued + product * jnp.where(inside, ahead(accrued, steps), 0.0)
        product = product * jnp.where(inside, ahead(product, steps), 1.0)
        steps *= 2
    accrued_ref[...] = accrued[:1]
    product_ref[...] = product[:1]
    for index in range(peers):
        heads_ref[index, 0:1, :] = jnp.broadcast_to(accrued[:1, :1], (1, owned))
        heads_ref[index, 1:2, :] = jnp.broadcast_to(product[:1, :1], (1, owned))


def finish_kernel(heads_ref, accrued_ref, product_ref, out_ref):
    here = lax.axis_index("batch")
    incoming = jnp.zeros((1, heads_ref.shape[2]), jnp.float32)
    for source in range(heads_ref.shape[0] - 1, 0, -1):
        passed = heads_ref[source, 0:1, :] + heads_ref[source, 1:2, :] * incoming
        incoming = jnp.where(source > here, passed, incoming)
    out_ref[...] = accrued_ref[...] + product_ref[...] * incoming


def finish(grid, parts, values, rewards, ref_logprob, segment_end):
    owned = values.shape[1]
    parts = lax.all_to_all(parts, ("batch", "vocab"), split_axis=0, concat_axis=0, tiled=True)
    row = jax.ShapeDtypeStruct((1, owned), jnp.float32)
    heads = jax.ShapeDtypeStruct((grid.peers, 2, owned), jnp.float32)
    logprob, heads, accrued, product = pl.pallas_call(
        lambda *refs: tail_kernel(grid, *refs),
        out_shape=(row, heads, row, row),
        in_specs=[VMEM] * 5,
        out_specs=(VMEM,) * 4,
        name="tail",
    )(parts, values, rewards, ref_logprob, segment_end)
    heads = lax.all_to_all(heads, "batch", split_axis=0, concat_axis=0, tiled=True)
    advantages = pl.pallas_call(
        finish_kernel,
        out_shape=row,
        in_specs=[VMEM] * 3,
        out_specs=VMEM,
        name="finish",
    )(heads, accrued, product)
    return logprob[0], advantages[0]


def per_device(
    grid, hidden, exit_layer, exit_gains, unembed, targets, values, rewards, ref_logprob, segment_end
):
    owned, width = hidden.shape
    half_rows = owned // 2
    normed, held = pl.pallas_call(
        lambda *refs: normalize_kernel(grid, *refs),
        out_shape=(
            jax.ShapeDtypeStruct((owned, width), jnp.bfloat16),
            jax.ShapeDtypeStruct((half_rows, width), jnp.bfloat16),
        ),
        in_specs=[VMEM] * 3,
        out_specs=(VMEM, VMEM),
        compiler_params=pltpu.CompilerParams(vmem_limit_bytes=16*MIB),
        name="normalize",
    )(hidden, exit_layer[None], exit_gains)
    ids = targets.reshape(grid.planes, 1, CORES * owned)
    weights = pl.pallas_call(
        load_kernel,
        out_shape=pltpu.VMEM(unembed.T.shape, unembed.dtype),
        in_specs=[ANY],
        out_specs=VMEM,
        scratch_shapes=[pltpu.SemaphoreType.DMA],
        compiler_params=pltpu.CompilerParams(vmem_limit_bytes=2 * MIB),
        name="load",
    )(unembed.T)
    parts = None
    values = values[None]
    twin = grid.twin(normed)
    above, other = grid.up(held), None
    for step in range(grid.planes):
        if step == 0:
            pieces = [
                (lambda core, half: core * owned, normed),
                (lambda core, half: (1 - core) * owned, twin),
            ]
            ahead, weights = lax.optimization_barrier((above, weights))
        else:
            other, parts = lax.optimization_barrier((other, parts))
            pieces = [
                (lambda core, half: core * owned + half * half_rows, held),
                (lambda core, half: core * owned + (1 - half) * half_rows, other),
                (lambda core, half: (1 - core) * owned + half * half_rows, twin),
                (lambda core, half: (1 - core) * owned + (1 - half) * half_rows, grid.twin(other)),
            ]
            if step + 1 < grid.planes:
                ahead, parts = lax.optimization_barrier((above, parts))
        if step + 1 < grid.planes:
            held = ahead
            other = grid.along_y(held) if step % 2 else grid.along_x(held)
            twin = grid.twin(held)
            if step + 2 < grid.planes:
                above = grid.up(held)
        first, last = step == 0, step == grid.planes - 1
        result = score(grid, step, pieces, ids, weights, parts, values, first, last)
        parts = result
    return finish(
        grid, parts, values, rewards[None], ref_logprob[None], segment_end[None]
    )


def solution(mesh):
    grid = Grid(mesh)
    placed = (
        P("batch", None),
        P("batch"),
        P(),
        P(None, ("batch", "vocab")),
        P(),
        P("batch"),
        P("batch"),
        P("batch"),
        P("batch"),
    )
    return jax.shard_map(
        lambda *arrays: per_device(grid, *arrays),
        mesh=mesh,
        in_specs=placed,
        out_specs=(P("batch"), P("batch")),
        check_vma=False,
    )
```

time: 664 us -> 107 us (0.16)
  loops' own time: 242 us -> 0 us
  local copies, waits for them, and re-layouts: 187 us -> 2.79 us
  waiting for transfers between devices: 104 us -> 17.5 us
  Pallas kernels: 0 us -> 54.9 us
  matrix products: 48.5 us -> 0 us
  starting transfers between devices: 39.4 us -> 11.1 us
  between operations: 14.1 us -> 0.72 us
  other arithmetic: 7.76 us -> 0 us
    another operation x4 -> x0, loops' own time: 242 us -> none  [the longest x1 237 us: per_device(): lax.scan(backward, (jnp.zeros((), jnp.float32), jnp.ones((), jnp.float32)...]
    dynamic_slice x259 -> x0, local copies, waits for them, and re-layouts: 155 us -> none  [the longest x256 155 us: per_device(): lax.scan(backward, (jnp.zeros((), jnp.float32), jnp.ones((), jnp.float32)...]
    all_gather x1 -> x0, waiting for transfers between devices: 83.9 us -> none  [per_device(): gathered = lax.all_gather(normed, 'batch', axis=0, tiled=True)]
    pallas_call x0 -> x8, Pallas kernels: none -> 54.9 us  [the longest x4 39.4 us: score(): pl.pallas_call(lambda *refs: score_kernel(grid, step, offsets, first, las...]
    dot_general x3 -> x0, matrix products: 48.5 us -> none  [the longest x2 45.2 us: score_block(): logits = jnp.dot(rows_block, unembed, preferred_element_type=jnp.float32)]
    dynamic_update_slice x262 -> x0, local copies, waits for them, and re-layouts: 29.6 us -> none  [the longest x256 29.4 us: per_device(): lax.scan(backward, (jnp.zeros((), jnp.float32), jnp.ones((), jnp.float32)...]
    all_to_all x0 -> x2, blocking collectives: none -> 19.1 us  [the longest x1 9.75 us: finish(): lax.all_to_all(heads, 'batch', split_axis=0, concat_axis=0, tiled=True)]
    ppermute x8 -> x13, starting transfers between devices: 28.2 us -> 11.1 us  [send(): return lax.ppermute(array, ('batch', 'vocab'), self.moves(target))]
  transfers between devices with their start and end apart: 12 -> 13, of which waited for: 10 -> 7; matrix products, arithmetic and copies ran while one was open for 0% -> 0% of each run, Pallas kernels for 0% -> 38%
where the time goes in v1:
time: 107 us; the launch traced here: 106 us
  Pallas kernels  54.9 us (51%)
  blocking collectives  19.1 us (18%)
  waiting for transfers between devices  17.5 us (16%)
  starting transfers between devices  11.1 us (10%)
  local copies, waits for them, and re-layouts  2.79 us (3%)
    pallas_call x4, Pallas kernels, score(): pl.pallas_call(lambda *refs: score_kernel(grid, step, offsets, first, las...  39.4 us
    ppermute x13, waiting for transfers between devices, send(): return lax.ppermute(array, ('batch', 'vocab'), self.moves(target))  17.5 us
    ppermute x13, starting transfers between devices, send(): return lax.ppermute(array, ('batch', 'vocab'), self.moves(target))  11.1 us
    pallas_call x1, Pallas kernels, per_device(): pl.pallas_call(load_kernel, out_shape=pltpu.VMEM(unembed.T.shape, unembed...  10.4 us
    all_to_all x1, blocking collectives, finish(): lax.all_to_all(heads, 'batch', split_axis=0, concat_axis=0, tiled=True)  9.75 us
    all_to_all x1, blocking collectives, finish(): lax.all_to_all(parts, ('batch', 'vocab'), split_axis=0, concat_axis=0, ti...  9.32 us
    unnamed x10, local copies, waits for them, and re-layouts  2.79 us
  transfers between devices with their start and end apart: 13, of which 7 were waited for; matrix products, arithmetic and copies ran while one was open for 0% of the time, Pallas kernels for 38%

profile of v1, /device:TPU:1, one launch (start us, length us, event | category | flops | bytes accessed | tf_op | source)
XLA Modules:
  0.0 106.0 jit_solution(9624602311837590602)
XLA Ops:
  0.6 1.2 %copy-done = bf16[128,4096]{1,0:T(8,128)(2,1)S(1)} copy-done((bf16[128,4096]{1,0:T(8,128)(2,1)S(1)}, bf16[128,4096]{1,0:T(8,128)(2,1)}, u32[]{:S(2)}) %copy-start) | copy-done | bytes 1048600
  1.9 0.9 copy-done.1
  2.8 0.7 copy-done.4
  3.4 1.8 %normalize.1 = (bf16[128,4096]{1,0:T(8,128)(2,1)S(1)}, bf16[64,4096]{1,0:T(8,128)(2,1)S(1)}) custom-call(bf16[128,4096]{1,0:T(8,128)(2,1)S(1)} %copy-done, s32[1,128]{1,0:T(1,128)S(1)} %bitcast.15, f32[8,4096]{1,0:T(8,128)S(1)} %copy-done.1), custom_call_target="tpu_custom_call" | custom-call | tf_op jit(solution)/shard_map/normalize/pallas_call | solution.py:282
  5.2 0.1 collective-permute-start.3
  5.3 2.8 %collective-permute-start = (bf16[64,4096]{1,0:T(8,128)(2,1)S(1)}, bf16[64,4096]{1,0:T(8,128)(2,1)S(1)}, u32[]{:S(2)}, u32[]{:S(2)}) collective-permute-start(bf16[64,4096]{1,0:T(8,128)(2,1)S(1)} %get-tuple-element.20), channel_id=1, source_target_pairs={{0,8},{1,9},{2,10},{3,11},{4,12},{5,13},{6,14},{7,15},{8,16},{9,17... | collective-permute-start | bytes 1572872 | tf_op jit(solution)/shard_map/ppermute | solution.py:38
  8.1 10.4 %load.1.refs_1_ = bf16[4008,4096]{1,0:T(8,128)(2,1)S(1)} custom-call(bf16[4008,4096]{1,0:T(8,128)(2,1)} %bitcast.16), custom_call_target="tpu_custom_call" | custom-call | tf_op jit(solution)/shard_map/load/pallas_call | solution.py:294
  18.5 3.9 %collective-permute-done.refs_3_ = bf16[64,4096]{1,0:T(8,128)(2,1)S(1)} collective-permute-done((bf16[64,4096]{1,0:T(8,128)(2,1)S(1)}, bf16[64,4096]{1,0:T(8,128)(2,1)S(1)}, u32[]{:S(2)}, u32[]{:S(2)}) %collective-permute-start) | collective-permute-done | bytes 524320 | tf_op jit(solution)/shard_map/ppermute | solution.py:38
  22.3 0.6 collective-permute-start.6
  23.0 1.2 %collective-permute-start.2 = (bf16[64,4096]{1,0:T(8,128)(2,1)S(1)}, bf16[64,4096]{1,0:T(8,128)(2,1)S(1)}, u32[]{:S(2)}, u32[]{:S(2)}) collective-permute-start(bf16[64,4096]{1,0:T(8,128)(2,1)S(1)} %collective-permute-done.refs_3_), channel_id=1, source_target_pairs={{0,1},{1,0},{2,3},{3,2},{4,5},{5,4},{6,7},{7,6},{8,9},{9,8},{10,11... | collective-permute-start | bytes 1572872 | tf_op jit(solution)/shard_map/ppermute | solution.py:38
  24.2 9.7 %score0.1.refs_2_ = f32[4,3,256]{2,1,0:T(4,128)S(1)} custom-call(s32[4,1,256]{2,1,0:T(1,128)S(1)} %bitcast.9, bf16[4008,4096]{1,0:T(8,128)(2,1)S(1)} %load.1.refs_1_, bf16[128,4096]{1,0:T(8,128)(2,1)S(1)} %get-tuple-element.23.refs_2_, bf16[128,4096]{1,0:T(8,128)(2,1)S(1)} %collective-permute-done.3.refs_3_), custom_call_target="tpu_custom_call" | custom-call | flops 8405385216 | tf_op jit(solution)/shard_map/score0/pallas_call | solution.py:184
  33.9 0.0 copy-start.3
  33.9 2.5 %collective-permute-done.2.refs_4_ = bf16[64,4096]{1,0:T(8,128)(2,1)S(1)} collective-permute-done((bf16[64,4096]{1,0:T(8,128)(2,1)S(1)}, bf16[64,4096]{1,0:T(8,128)(2,1)S(1)}, u32[]{:S(2)}, u32[]{:S(2)}) %collective-permute-start.2) | collective-permute-done | bytes 524320 | tf_op jit(solution)/shard_map/ppermute | solution.py:38
  36.5 0.9 collective-permute-start.7
  37.3 1.9 %collective-permute-done.1.refs_3_ = bf16[64,4096]{1,0:T(8,128)(2,1)S(1)} collective-permute-done((bf16[64,4096]{1,0:T(8,128)(2,1)S(1)}, bf16[64,4096]{1,0:T(8,128)(2,1)S(1)}, u32[]{:S(2)}, u32[]{:S(2)}) %collective-permute-start.1) | collective-permute-done | bytes 524320 | tf_op jit(solution)/shard_map/ppermute | solution.py:38
  39.2 1.1 %collective-permute-start.9 = (bf16[64,4096]{1,0:T(8,128)(2,1)S(1)}, bf16[64,4096]{1,0:T(8,128)(2,1)S(1)}, u32[]{:S(2)}, u32[]{:S(2)}) collective-permute-start(bf16[64,4096]{1,0:T(8,128)(2,1)S(1)} %collective-permute-done.1.refs_3_), channel_id=1, source_target_pairs={{0,4},{1,5},{2,6},{3,7},{4,0},{5,1},{6,2},{7,3},{8,12},{9,13},{10,... | collective-permute-start | bytes 1572872 | tf_op jit(solution)/shard_map/ppermute | solution.py:38
  40.3 1.2 %collective-permute-start.5 = (bf16[64,4096]{1,0:T(8,128)(2,1)S(1)}, bf16[64,4096]{1,0:T(8,128)(2,1)S(1)}, u32[]{:S(2)}, u32[]{:S(2)}) collective-permute-start(bf16[64,4096]{1,0:T(8,128)(2,1)S(1)} %collective-permute-done.1.refs_3_), channel_id=1, source_target_pairs={{0,2},{1,3},{2,0},{3,1},{4,6},{5,7},{6,4},{7,5},{8,10},{9,11},{10,... | collective-permute-start | bytes 1572872 | tf_op jit(solution)/shard_map/ppermute | solution.py:38
  41.6 9.7 %score1.1.refs_2_ = f32[4,3,256]{2,1,0:T(4,128)S(1)} custom-call(s32[4,1,256]{2,1,0:T(1,128)S(1)} %bitcast.10, bf16[4008,4096]{1,0:T(8,128)(2,1)S(1)} %load.1.refs_1_, f32[4,3,256]{2,1,0:T(4,128)S(1)} %score0.1.refs_2_, bf16[64,4096]{1,0:T(8,128)(2,1)S(1)} %collective-permute-done.refs_3_, bf16[64,4096]{1,0:T(8,128)(2,1)S(1)} %collective-permute-done.2.refs_4_, ...), custom_call_target="tpu_custom_call" | custom-call | flops 8405385216 | tf_op jit(solution)/shard_map/score1/pallas_call | solution.py:184
  51.3 2.5 %collective-permute-done.5.refs_4_ = bf16[64,4096]{1,0:T(8,128)(2,1)S(1)} collective-permute-done((bf16[64,4096]{1,0:T(8,128)(2,1)S(1)}, bf16[64,4096]{1,0:T(8,128)(2,1)S(1)}, u32[]{:S(2)}, u32[]{:S(2)}) %collective-permute-start.5) | collective-permute-done | bytes 524320 | tf_op jit(solution)/shard_map/ppermute | solution.py:38
  53.8 0.9 collective-permute-start.10
  54.7 1.9 %collective-permute-done.4.refs_4_ = bf16[64,4096]{1,0:T(8,128)(2,1)S(1)} collective-permute-done((bf16[64,4096]{1,0:T(8,128)(2,1)S(1)}, bf16[64,4096]{1,0:T(8,128)(2,1)S(1)}, u32[]{:S(2)}, u32[]{:S(2)}) %collective-permute-start.4) | collective-permute-done | bytes 524320 | tf_op jit(solution)/shard_map/ppermute | solution.py:38
  56.6 1.1 %collective-permute-start.11 = (bf16[64,4096]{1,0:T(8,128)(2,1)S(1)}, bf16[64,4096]{1,0:T(8,128)(2,1)S(1)}, u32[]{:S(2)}, u32[]{:S(2)}) collective-permute-start(bf16[64,4096]{1,0:T(8,128)(2,1)S(1)} %collective-permute-done.4.refs_4_), channel_id=1, source_target_pairs={{0,4},{1,5},{2,6},{3,7},{4,0},{5,1},{6,2},{7,3},{8,12},{9,13},{10,... | collective-permute-start | bytes 1572872 | tf_op jit(solution)/shard_map/ppermute | solution.py:38
  57.7 0.3 collective-permute-start.8
  58.0 9.9 %score2.1.refs_2_ = f32[4,3,256]{2,1,0:T(4,128)S(1)} custom-call(s32[4,1,256]{2,1,0:T(1,128)S(1)} %bitcast.11, bf16[4008,4096]{1,0:T(8,128)(2,1)S(1)} %load.1.refs_1_, f32[4,3,256]{2,1,0:T(4,128)S(1)} %score1.1.refs_2_, bf16[64,4096]{1,0:T(8,128)(2,1)S(1)} %collective-permute-done.1.refs_3_, bf16[64,4096]{1,0:T(8,128)(2,1)S(1)} %collective-permute-done.5.refs_4_, ...), custom_call_target="tpu_custom_call" | custom-call | flops 8405385216 | tf_op jit(solution)/shard_map/score2/pallas_call | solution.py:184
  67.9 3.3 %collective-permute-done.8.refs_5_ = bf16[64,4096]{1,0:T(8,128)(2,1)S(1)} collective-permute-done((bf16[64,4096]{1,0:T(8,128)(2,1)S(1)}, bf16[64,4096]{1,0:T(8,128)(2,1)S(1)}, u32[]{:S(2)}, u32[]{:S(2)}) %collective-permute-start.8) | collective-permute-done | bytes 524320 | tf_op jit(solution)/shard_map/ppermute | solution.py:38
  71.2 0.9 collective-permute-start.12
  72.1 1.5 %collective-permute-done.12.refs_7_ = bf16[64,4096]{1,0:T(8,128)(2,1)S(1)} collective-permute-done((bf16[64,4096]{1,0:T(8,128)(2,1)S(1)}, bf16[64,4096]{1,0:T(8,128)(2,1)S(1)}, u32[]{:S(2)}, u32[]{:S(2)}) %collective-permute-start.12) | collective-permute-done | bytes 524320 | tf_op jit(solution)/shard_map/ppermute | solution.py:38
  73.6 10.0 %score3.1 = f32[32,4,128]{2,1,0:T(4,128)S(1)} custom-call(s32[4,1,256]{2,1,0:T(1,128)S(1)} %bitcast.12, bf16[4008,4096]{1,0:T(8,128)(2,1)S(1)} %load.1.refs_1_, f32[4,3,256]{2,1,0:T(4,128)S(1)} %score2.1.refs_2_, f32[1,128]{1,0:T(1,128)S(1)} %bitcast.14, bf16[64,4096]{1,0:T(8,128)(2,1)S(1)} %collective-permute-done.4.refs_4_, ...), custom_call_target="tpu_custom_call" | custom-call | flops 8405385216 | tf_op jit(solution)/shard_map/score3/pallas_call | solution.py:184
  83.6 9.3 %all_to_all.10.refs_0_ = f32[32,4,128]{2,1,0:T(4,128)} all-to-all(f32[32,4,128]{2,1,0:T(4,128)S(1)} %score3.1), channel_id=1, replica_groups=mesh['batch'=8,'vocab'=4] {'batch','vocab'}, dimensions={0} | all-to-all | bytes 131072 | tf_op jit(solution)/shard_map/all_to_all | solution.py:256
  93.0 2.1 %tail.1 = (f32[1,128]{1,0:T(1,128)}, f32[8,2,128]{2,1,0:T(2,128)}, f32[1,128]{1,0:T(1,128)}, f32[1,128]{1,0:T(1,128)}) custom-call(f32[32,4,128]{2,1,0:T(4,128)} %all_to_all.10.refs_0_, f32[1,128]{1,0:T(1,128)} %bitcast.13, f32[1,128]{1,0:T(1,128)} %bitcast.17, f32[1,128]{1,0:T(1,128)} %bitcast.18, s32[1,128]{1,0:T(1,128)} %bitcast.19), custom_call_target="tpu_custom_call" | custom-call | tf_op jit(solution)/shard_map/tail/pallas_call | solution.py:259
  95.1 9.7 %all_to_all.11.heads_ref = f32[8,2,128]{2,1,0:T(2,128)} all-to-all(f32[8,2,128]{2,1,0:T(2,128)} %get-tuple-element.35), channel_id=1, replica_groups=mesh['batch'=8,'vocab'=4] {'batch'}, dimensions={0} | all-to-all | bytes 16384 | tf_op jit(solution)/shard_map/all_to_all | solution.py:266
  104.8 1.2 %finish.1 = f32[1,128]{1,0:T(1,128)} custom-call(f32[8,2,128]{2,1,0:T(2,128)} %all_to_all.11.heads_ref, f32[1,128]{1,0:T(1,128)} %get-tuple-element.36.accrued_ref, f32[1,128]{1,0:T(1,128)} %get-tuple-element.37.product_ref), custom_call_target="tpu_custom_call" | custom-call | tf_op jit(solution)/shard_map/finish/pallas_call | solution.py:267
  (14 shorter events, 0.0 us)
Async XLA Ops:
  0.6 1.2 %copy-start = (bf16[128,4096]{1,0:T(8,128)(2,1)S(1)}, bf16[128,4096]{1,0:T(8,128)(2,1)}, u32[]{:S(2)}) copy-start(bf16[128,4096]{1,0:T(8,128)(2,1)} %refs_0_.1) | copy-start | bytes 3145732
  1.9 0.9 copy-start.1
  2.8 0.7 copy-start.4
  5.2 19.0 %collective-permute-start.3 = (bf16[128,4096]{1,0:T(8,128)(2,1)S(1)}, bf16[128,4096]{1,0:T(8,128)(2,1)S(1)}, u32[]{:S(2)}, u32[]{:S(2)}) collective-permute-start(bf16[128,4096]{1,0:T(8,128)(2,1)S(1)} %get-tuple-element.23.refs_2_), channel_id=1, source_target_pairs={{0,4},{1,5},{2,6},{3,7},{4,0},{5,1},{6,2},{7,3},{8,12},{9,13},{10,... | collective-permute-start | bytes 3145736 | tf_op jit(solution)/shard_map/ppermute | solution.py:38
  5.3 17.0 %collective-permute-start = (bf16[64,4096]{1,0:T(8,128)(2,1)S(1)}, bf16[64,4096]{1,0:T(8,128)(2,1)S(1)}, u32[]{:S(2)}, u32[]{:S(2)}) collective-permute-start(bf16[64,4096]{1,0:T(8,128)(2,1)S(1)} %get-tuple-element.20), channel_id=1, source_target_pairs={{0,8},{1,9},{2,10},{3,11},{4,12},{5,13},{6,14},{7,15},{8,16},{9,17... | collective-permute-start | bytes 1572872 | tf_op jit(solution)/shard_map/ppermute | solution.py:38
  8.1 16.1 %copy-start.2 = (s32[1024]{0:T(1024)S(1)}, s32[1024]{0:T(1024)}, u32[]{:S(2)}) copy-start(s32[1024]{0:T(1024)} %param.13) | copy-start | bytes 12292
  22.3 19.2 %collective-permute-start.6 = (bf16[64,4096]{1,0:T(8,128)(2,1)S(1)}, bf16[64,4096]{1,0:T(8,128)(2,1)S(1)}, u32[]{:S(2)}, u32[]{:S(2)}) collective-permute-start(bf16[64,4096]{1,0:T(8,128)(2,1)S(1)} %collective-permute-done.refs_3_), channel_id=1, source_target_pairs={{0,4},{1,5},{2,6},{3,7},{4,0},{5,1},{6,2},{7,3},{8,12},{9,13},{10,... | collective-permute-start | bytes 1572872 | tf_op jit(solution)/shard_map/ppermute | solution.py:38
  23.0 13.5 %collective-permute-start.2 = (bf16[64,4096]{1,0:T(8,128)(2,1)S(1)}, bf16[64,4096]{1,0:T(8,128)(2,1)S(1)}, u32[]{:S(2)}, u32[]{:S(2)}) collective-permute-start(bf16[64,4096]{1,0:T(8,128)(2,1)S(1)} %collective-permute-done.refs_3_), channel_id=1, source_target_pairs={{0,1},{1,0},{2,3},{3,2},{4,5},{5,4},{6,7},{7,6},{8,9},{9,8},{10,11... | collective-permute-start | bytes 1572872 | tf_op jit(solution)/shard_map/ppermute | solution.py:38
  24.2 15.0 %collective-permute-start.1 = (bf16[64,4096]{1,0:T(8,128)(2,1)S(1)}, bf16[64,4096]{1,0:T(8,128)(2,1)S(1)}, u32[]{:S(2)}, u32[]{:S(2)}) collective-permute-start(bf16[64,4096]{1,0:T(8,128)(2,1)S(1)} %collective-permute-done.refs_3_), channel_id=1, source_target_pairs={{0,8},{1,9},{2,10},{3,11},{4,12},{5,13},{6,14},{7,15},{8,16},{9,17... | collective-permute-start | bytes 1572872 | tf_op jit(solution)/shard_map/ppermute | solution.py:38
  33.9 39.7 %copy-start.3 = (f32[128]{0:T(128)S(1)}, f32[128]{0:T(128)}, u32[]{:S(2)}) copy-start(f32[128]{0:T(128)} %param.14) | copy-start | bytes 1540
  36.5 5.1 %collective-permute-start.7 = (bf16[64,4096]{1,0:T(8,128)(2,1)S(1)}, bf16[64,4096]{1,0:T(8,128)(2,1)S(1)}, u32[]{:S(2)}, u32[]{:S(2)}) collective-permute-start(bf16[64,4096]{1,0:T(8,128)(2,1)S(1)} %collective-permute-done.2.refs_4_), channel_id=1, source_target_pairs={{0,4},{1,5},{2,6},{3,7},{4,0},{5,1},{6,2},{7,3},{8,12},{9,13},{10,... | collective-permute-start | bytes 1572872 | tf_op jit(solution)/shard_map/ppermute | solution.py:38
  39.2 18.8 %collective-permute-start.9 = (bf16[64,4096]{1,0:T(8,128)(2,1)S(1)}, bf16[64,4096]{1,0:T(8,128)(2,1)S(1)}, u32[]{:S(2)}, u32[]{:S(2)}) collective-permute-start(bf16[64,4096]{1,0:T(8,128)(2,1)S(1)} %collective-permute-done.1.refs_3_), channel_id=1, source_target_pairs={{0,4},{1,5},{2,6},{3,7},{4,0},{5,1},{6,2},{7,3},{8,12},{9,13},{10,... | collective-permute-start | bytes 1572872 | tf_op jit(solution)/shard_map/ppermute | solution.py:38
  40.3 13.5 %collective-permute-start.5 = (bf16[64,4096]{1,0:T(8,128)(2,1)S(1)}, bf16[64,4096]{1,0:T(8,128)(2,1)S(1)}, u32[]{:S(2)}, u32[]{:S(2)}) collective-permute-start(bf16[64,4096]{1,0:T(8,128)(2,1)S(1)} %collective-permute-done.1.refs_3_), channel_id=1, source_target_pairs={{0,2},{1,3},{2,0},{3,1},{4,6},{5,7},{6,4},{7,5},{8,10},{9,11},{10,... | collective-permute-start | bytes 1572872 | tf_op jit(solution)/shard_map/ppermute | solution.py:38
  41.6 15.0 %collective-permute-start.4 = (bf16[64,4096]{1,0:T(8,128)(2,1)S(1)}, bf16[64,4096]{1,0:T(8,128)(2,1)S(1)}, u32[]{:S(2)}, u32[]{:S(2)}) collective-permute-start(bf16[64,4096]{1,0:T(8,128)(2,1)S(1)} %collective-permute-done.1.refs_3_), channel_id=1, source_target_pairs={{0,8},{1,9},{2,10},{3,11},{4,12},{5,13},{6,14},{7,15},{8,16},{9,17... | collective-permute-start | bytes 1572872 | tf_op jit(solution)/shard_map/ppermute | solution.py:38
  53.8 4.2 %collective-permute-start.10 = (bf16[64,4096]{1,0:T(8,128)(2,1)S(1)}, bf16[64,4096]{1,0:T(8,128)(2,1)S(1)}, u32[]{:S(2)}, u32[]{:S(2)}) collective-permute-start(bf16[64,4096]{1,0:T(8,128)(2,1)S(1)} %collective-permute-done.5.refs_4_), channel_id=1, source_target_pairs={{0,4},{1,5},{2,6},{3,7},{4,0},{5,1},{6,2},{7,3},{8,12},{9,13},{10,... | collective-permute-start | bytes 1572872 | tf_op jit(solution)/shard_map/ppermute | solution.py:38
  56.6 15.5 %collective-permute-start.11 = (bf16[64,4096]{1,0:T(8,128)(2,1)S(1)}, bf16[64,4096]{1,0:T(8,128)(2,1)S(1)}, u32[]{:S(2)}, u32[]{:S(2)}) collective-permute-start(bf16[64,4096]{1,0:T(8,128)(2,1)S(1)} %collective-permute-done.4.refs_4_), channel_id=1, source_target_pairs={{0,4},{1,5},{2,6},{3,7},{4,0},{5,1},{6,2},{7,3},{8,12},{9,13},{10,... | collective-permute-start | bytes 1572872 | tf_op jit(solution)/shard_map/ppermute | solution.py:38
  57.7 13.5 %collective-permute-start.8 = (bf16[64,4096]{1,0:T(8,128)(2,1)S(1)}, bf16[64,4096]{1,0:T(8,128)(2,1)S(1)}, u32[]{:S(2)}, u32[]{:S(2)}) collective-permute-start(bf16[64,4096]{1,0:T(8,128)(2,1)S(1)} %collective-permute-done.4.refs_4_), channel_id=1, source_target_pairs={{0,1},{1,0},{2,3},{3,2},{4,5},{5,4},{6,7},{7,6},{8,9},{9,8},{10,11... | collective-permute-start | bytes 1572872 | tf_op jit(solution)/shard_map/ppermute | solution.py:38
  71.2 2.4 %collective-permute-start.12 = (bf16[64,4096]{1,0:T(8,128)(2,1)S(1)}, bf16[64,4096]{1,0:T(8,128)(2,1)S(1)}, u32[]{:S(2)}, u32[]{:S(2)}) collective-permute-start(bf16[64,4096]{1,0:T(8,128)(2,1)S(1)} %collective-permute-done.8.refs_5_), channel_id=1, source_target_pairs={{0,4},{1,5},{2,6},{3,7},{4,0},{5,1},{6,2},{7,3},{8,12},{9,13},{10,... | collective-permute-start | bytes 1572872 | tf_op jit(solution)/shard_map/ppermute | solution.py:38

commit v2 on v1

v2 whole, which is shorter than its diff:
```python
import math

import jax
import jax.numpy as jnp
from jax import lax
from jax.experimental import pallas as pl
from jax.experimental.pallas import tpu as pltpu
from jax.sharding import PartitionSpec as P


epsilon_norm = 1e-05
discount = 1.0
trace_decay = 0.999
penalty_weight = 0.1
CORES = 2
LOWEST = float(jnp.finfo(jnp.float32).min)
VMEM = pl.BlockSpec(memory_space=pltpu.VMEM)
ANY = pl.BlockSpec(memory_space=pl.ANY)
HBM = pl.BlockSpec(memory_space=pltpu.HBM)
MIB = 2**20


class Grid:
    def __init__(self, mesh):
        self.peers, self.groups = mesh.shape["batch"], mesh.shape["vocab"]
        self.planes = self.peers // CORES
        self.side = math.isqrt(self.groups)

    def moves(self, target):
        pairs = []
        for b in range(self.peers):
            for v in range(self.groups):
                z, c, y, x = target(b // CORES, b % CORES, v // self.side, v % self.side)
                pairs.append((b * self.groups + v, (z * CORES + c) * self.groups + y * self.side + x))
        return pairs

    def send(self, array, target):
        return lax.ppermute(array, ("batch", "vocab"), self.moves(target))

    def twin(self, array):
        return self.send(array, lambda z, c, y, x: (z, 1 - c, y, x))

    def line(self, position):
        position %= self.planes
        return 2 * position - 1 if 0 < 2 * position <= self.planes else 2 * (self.planes - position) % self.planes

    def up(self, array, steps=1):
        where = {self.line(position): position for position in range(self.planes)}
        return self.send(array, lambda z, c, y, x: (self.line(where[z] + steps), c, y, x))

    def origin(self, plane, steps):
        if steps == 0:
            return plane
        count = self.planes
        even = lax.rem(count - lax.div(plane, 2), count)
        position = jnp.where(lax.rem(plane, 2) == 1, lax.div(plane + 1, 2), even)
        position = lax.rem(position - steps + count, count)
        low = (position > 0) & (2 * position <= count)
        return jnp.where(low, 2 * position - 1, lax.rem(2 * (count - position), count))

    def across(self, array, down, along):
        side = self.side
        return self.send(array, lambda z, c, y, x: (z, c, (y + down) % side, (x + along) % side))

    def along_x(self, array):
        return self.send(array, lambda z, c, y, x: (z, c, y, x ^ 1))

    def along_y(self, array):
        return self.send(array, lambda z, c, y, x: (z, c, y ^ 1, x))

    def place(self):
        b, v = lax.axis_index("batch"), lax.axis_index("vocab")
        half = lax.rem(lax.div(v, self.side) + lax.rem(v, self.side), 2)
        return lax.div(b, CORES), lax.rem(b, CORES), half


def normalize_kernel(grid, halved, hidden_hbm, layers_hbm, gains_hbm, out_ref,
                     states_ref, layers_ref, wide_ref, gains_ref, sem):
    rows = out_ref.shape[0]
    block = 16
    chunk = 32
    exits = gains_ref.shape[0]
    start = pl.multiple_of(grid.place()[2] * rows, rows) if halved else 0
    small = [
        pltpu.make_async_copy(layers_hbm, layers_ref, sem.at[0]),
        pltpu.make_async_copy(gains_hbm, gains_ref, sem.at[1]),
    ]
    large = []
    for index in range(rows // chunk):
        large.append(
            pltpu.make_async_copy(
                hidden_hbm.at[pl.ds(start + index * chunk, chunk)],
                states_ref.at[pl.ds(index * chunk, chunk)],
                sem.at[2 + index],
            )
        )
    for copy in small + large:
        copy.start()
    small[0].wait()
    owned = layers_ref.shape[1]
    wide_ref[...] = jnp.broadcast_to(layers_ref[...], (owned, owned)).astype(jnp.float32).T
    small[1].wait()
    for index, copy in enumerate(large):
        copy.wait()

        def body(turn, carry):
            begin = pl.multiple_of(index * chunk + turn * block, block)
            part = pl.ds(begin, block)
            states = states_ref[part, :].astype(jnp.float32)
            mean = jnp.sum(states * states, axis=1, keepdims=True) / states.shape[1]
            inverse = lax.rsqrt(mean + epsilon_norm)
            layer = wide_ref[pl.ds(pl.multiple_of(start + begin, block), block), :1]
            scaling = jnp.broadcast_to(gains_ref[0:1, :], states.shape)
            for exit_index in range(1, exits):
                scaling = jnp.where(
                    layer == float(exit_index), gains_ref[exit_index : exit_index + 1, :], scaling
                )
            out_ref[part, :] = (states * inverse * scaling).astype(out_ref.dtype)
            return carry

        lax.fori_loop(0, chunk // block, body, 0)


def normalize(grid, halved, hidden, layers, gains):
    owned, width = hidden.shape
    rows = owned // 2 if halved else owned
    return pl.pallas_call(
        lambda *refs: normalize_kernel(grid, halved, *refs),
        out_shape=jax.ShapeDtypeStruct((rows, width), jnp.bfloat16),
        in_specs=[HBM] * 3,
        out_specs=VMEM,
        scratch_shapes=[
            pltpu.VMEM((rows, width), hidden.dtype),
            pltpu.VMEM(layers.shape, layers.dtype),
            pltpu.VMEM((owned, owned), jnp.float32),
            pltpu.VMEM(gains.shape, gains.dtype),
            pltpu.SemaphoreType.DMA((2 + rows // 32,)),
        ],
        compiler_params=pltpu.CompilerParams(vmem_limit_bytes=60 * MIB),
        name="share" if halved else "normalize",
    )(hidden, layers, gains)


def spans(rows, target):
    count = max(1, round(rows / target))
    size = -(-rows // (count * 16)) * 16
    return [(begin, min(size, rows - begin)) for begin in range(0, rows, size)]


def tally(logits, begin, wanted, carry):
    old, total, pick = carry
    place = lax.broadcasted_iota(jnp.int32, logits.shape, 0) + begin
    new = jnp.maximum(old, jnp.max(logits, axis=0, keepdims=True))
    total = total * jnp.exp(old - new) + jnp.sum(jnp.exp(logits - new), axis=0, keepdims=True)
    pick = pick + jnp.sum(jnp.where(place == wanted, logits, 0.0), axis=0, keepdims=True)
    return new, total, pick


def product(weights, states):
    return lax.dot_general(
        weights, states, (((1,), (1,)), ((), ())), preferred_element_type=jnp.float32
    )


def score_kernel(grid, step, pieces, first, *refs):
    refs = list(refs)
    ids_ref, weights_in = refs.pop(0), refs.pop(0)
    parts_in = None if first else refs.pop(0)
    piece_refs = [refs.pop(0) for _ in pieces]
    parts_ref = refs.pop(0)
    weights_ref = weights_in
    states_ref, piece_sem = refs.pop(0), refs.pop(0)
    rows = weights_ref.shape[0]
    plane, core, half = grid.place()
    source = grid.origin(plane, step)
    copies = []
    for index, (piece, ref) in enumerate(zip(pieces, piece_refs)):
        offset = pl.multiple_of(piece(core, half), ref.shape[0])
        copies.append(
            pltpu.make_async_copy(ref, states_ref.at[pl.ds(offset, ref.shape[0])], piece_sem.at[index])
        )
    for copy in copies:
        copy.start()
    blocks = spans(rows, 1336)
    for copy in copies:
        copy.wait()
    start = (lax.axis_index("batch") * grid.groups + lax.axis_index("vocab")) * rows
    wanted = ids_ref[source] - start
    tokens = states_ref.shape[0]
    carry = (
        jnp.full((1, tokens), LOWEST, jnp.float32),
        jnp.zeros((1, tokens), jnp.float32),
        jnp.zeros((1, tokens), jnp.float32),
    )
    pending = None
    for begin, size in blocks:
        logits = product(weights_ref[begin : begin + size, :], states_ref[...])
        if pending is not None:
            carry = tally(*pending, wanted, carry)
        pending = (logits, begin)
    carry = tally(*pending, wanted, carry)
    if not first:
        parts_ref[...] = parts_in[...]
    for index in range(3):
        parts_ref[source, index : index + 1, :] = carry[index]


def score(grid, step, pieces, ids, weights, parts, first):
    owned = pieces[0][1].shape[0] if first else pieces[0][1].shape[0] * 2
    width = weights.shape[1]
    rows = weights.shape[0]
    tokens = owned * CORES
    out_shape = jax.ShapeDtypeStruct((grid.planes, 3, tokens), jnp.float32)
    args = [ids, weights]
    specs = [VMEM, VMEM]
    if not first:
        args.append(parts)
        specs.append(VMEM)
    args += [array for _, array in pieces]
    specs += [HBM] * len(pieces)
    scratch = [
        pltpu.VMEM((tokens, width), jnp.bfloat16),
        pltpu.SemaphoreType.DMA((len(pieces),)),
    ]
    out_specs = VMEM
    limit = 8
    offsets = [offset for offset, _ in pieces]
    return pl.pallas_call(
        lambda *refs: score_kernel(grid, step, offsets, first, *refs),
        out_shape=out_shape,
        in_specs=specs,
        out_specs=out_specs,
        scratch_shapes=scratch,
        compiler_params=pltpu.CompilerParams(vmem_limit_bytes=limit * MIB),
        cost_estimate=pl.CostEstimate(
            flops=2 * rows * tokens * width, transcendentals=rows * tokens, bytes_accessed=0
        ),
    )(*args)


def load_kernel(weights_in, weights_ref, sem):
    copy = pltpu.make_async_copy(weights_in, weights_ref, sem)
    copy.start()
    copy.wait()


def joined(sources):
    larger = sources[0][0]
    for source in sources[1:]:
        larger = jnp.maximum(larger, source[0])
    total = sum(source[1] * jnp.exp(source[0] - larger) for source in sources)
    return larger, total, sum(source[2] for source in sources)


def triple(ref, count):
    return [ref[index * count : (index + 1) * count, :] for index in range(3)]


def brought(kernel, count):
    def body(*refs):
        held, sem = refs[len(refs) - count - 1 : -1], refs[-1]
        copies = [
            pltpu.make_async_copy(ref, to, sem.at[index])
            for index, (ref, to) in enumerate(zip(refs[:count], held))
        ]
        for copy in copies:
            copy.start()
        for copy in copies:
            copy.wait()
        kernel(*held, *refs[count : len(refs) - count - 1])

    return body


def gather_call(kernel, arrays, out_shape, scratch):
    many = isinstance(out_shape, tuple)
    held = [pltpu.VMEM(array.shape, array.dtype) for array in arrays]
    return pl.pallas_call(
        brought(kernel, len(arrays)),
        out_shape=out_shape,
        in_specs=[ANY] * len(arrays),
        out_specs=(VMEM,) * len(out_shape) if many else VMEM,
        scratch_shapes=scratch + held + [pltpu.SemaphoreType.DMA((len(arrays),))],
        compiler_params=pltpu.CompilerParams(vmem_limit_bytes=4 * MIB),
    )(*arrays)


def pack_kernel(grid, *refs):
    parts, rows, out_ref = refs[: grid.groups], refs[grid.groups : -1], refs[-1]
    count = grid.planes
    merged = joined([[ref[:, index, :] for index in range(3)] for ref in parts])
    for index in range(3):
        out_ref[index * count : (index + 1) * count, :] = merged[index]
    tokens = out_ref.shape[1]
    owned = tokens // CORES
    core = grid.place()[1]
    lane = lax.broadcasted_iota(jnp.int32, (1, tokens), 1)
    mine = (lane >= core * owned) & (lane < core * owned + owned)
    for index, ref in enumerate(rows):
        row = ref[...].astype(jnp.float32)
        row = jnp.concatenate([row] * CORES, axis=1)
        out_ref[3 * count + index : 3 * count + index + 1, :] = jnp.where(mine, row, 0.0)


def pair_kernel(grid, mine_ref, other_ref, out_ref):
    count = grid.planes
    merged = joined([triple(mine_ref, count), triple(other_ref, count)])
    for index in range(3):
        out_ref[index * count : (index + 1) * count, :] = merged[index]
    out_ref[3 * count :, :] = mine_ref[3 * count :, :] + other_ref[3 * count :, :]


def tail_kernel(grid, *refs):
    count = grid.planes
    sources = refs[:count]
    logprob_out, advantage_out, rows_ref, logprob_ref, advantage_ref = refs[count:]
    peers, owned = logprob_ref.shape
    plane = grid.place()[0]
    larger, total, picked = joined([triple(ref, count) for ref in sources])
    logprob = picked - (larger + jnp.log(total))
    for group in range(count):
        for core in range(CORES):
            span = slice(core * owned, (core + 1) * owned)
            row = group * CORES + core
            logprob_ref[row : row + 1, :] = logprob[group : group + 1, span]
    for step, ref in enumerate(sources):
        source = grid.origin(plane, step)
        for core in range(CORES):
            span = slice(core * owned, (core + 1) * owned)
            rows_ref[source * CORES + core] = ref[3 * count :, span]
    rows_ref[peers] = jnp.zeros(rows_ref.shape[1:], jnp.float32)
    lane = lax.broadcasted_iota(jnp.int32, (peers, owned), 1)
    line = lax.broadcasted_iota(jnp.int32, (peers, owned), 0)
    logprob = logprob_ref[...]
    values = rows_ref[0:peers, 0, :]
    entering = jnp.broadcast_to(rows_ref[1 : peers + 1, 0, :][:, :1], (peers, owned))
    following = jnp.where(lane < owned - 1, pltpu.roll(values, owned - 1, 1), entering)
    keeping = 1.0 - rows_ref[0:peers, 3, :]
    shaped = rows_ref[0:peers, 1, :] - penalty_weight * (logprob - rows_ref[0:peers, 2, :])
    accrued = shaped + discount * following * keeping - values
    product = discount * trace_decay * keeping

    def doubled(accrued, product, place, extent, axis):
        steps = 1
        while steps < extent:
            inside = place < extent - steps
            later = jnp.where(inside, pltpu.roll(accrued, extent - steps, axis), 0.0)
            accrued = accrued + product * later
            product = product * jnp.where(inside, pltpu.roll(product, extent - steps, axis), 1.0)
            steps *= 2
        return accrued, product

    accrued, product = doubled(accrued, product, lane, owned, 1)
    heads = jnp.broadcast_to(accrued[:, :1], (peers, owned))
    rates = jnp.broadcast_to(product[:, :1], (peers, owned))
    heads = doubled(heads, rates, line, peers, 0)[0]
    incoming = jnp.where(line < peers - 1, pltpu.roll(heads, peers - 1, 0), 0.0)
    advantage_ref[...] = accrued + product * incoming
    here = lax.axis_index("batch")
    logprob_out[...] = logprob_ref[pl.ds(here, 1), :]
    advantage_out[...] = advantage_ref[pl.ds(here, 1), :]


def finish(grid, parts, rows):
    owned = rows[0].shape[1]
    tokens = owned * CORES
    shape = jax.ShapeDtypeStruct((3 * grid.planes + len(rows), tokens), jnp.float32)
    plane = [
        grid.across(parts, down, along)
        for down in range(grid.side)
        for along in range(grid.side)
        if down or along
    ]
    packed = gather_call(lambda *refs: pack_kernel(grid, *refs), [parts, *plane, *rows], shape, [])
    paired = gather_call(
        lambda *refs: pair_kernel(grid, *refs), [packed, grid.twin(packed)], shape, []
    )
    row = jax.ShapeDtypeStruct((1, owned), jnp.float32)
    planes = [paired] + [grid.up(paired, step) for step in range(1, grid.planes)]
    logprob, advantages = gather_call(
        lambda *refs: tail_kernel(grid, *refs),
        planes,
        (row, row),
        [
            pltpu.VMEM((grid.peers + 1, len(rows), owned), jnp.float32),
            pltpu.VMEM((grid.peers, owned), jnp.float32),
            pltpu.VMEM((grid.peers, owned), jnp.float32),
        ],
    )
    return logprob[0], advantages[0]


def per_device(
    grid, hidden, exit_layer, exit_gains, unembed, targets, values, rewards, ref_logprob, segment_end
):
    owned, _ = hidden.shape
    half_rows = owned // 2
    held = normalize(grid, True, hidden, exit_layer[None], exit_gains)
    hidden, held = lax.optimization_barrier((hidden, held))
    normed = normalize(grid, False, hidden, exit_layer[None], exit_gains)
    ids = targets.reshape(grid.planes, 1, CORES * owned)
    weights = pl.pallas_call(
        load_kernel,
        out_shape=pltpu.VMEM(unembed.T.shape, unembed.dtype),
        in_specs=[ANY],
        out_specs=VMEM,
        scratch_shapes=[pltpu.SemaphoreType.DMA],
        compiler_params=pltpu.CompilerParams(vmem_limit_bytes=2 * MIB),
        name="load",
    )(unembed.T)
    parts = None
    twin = grid.twin(normed)
    above = grid.up(held)
    other = None
    for step in range(grid.planes):
        if step == 0:
            pieces = [
                (lambda core, half: core * owned, normed),
                (lambda core, half: (1 - core) * owned, twin),
            ]
            ahead, weights = lax.optimization_barrier((above, weights))
        else:
            other, parts = lax.optimization_barrier((other, parts))
            pieces = [
                (lambda core, half: core * owned + half * half_rows, held),
                (lambda core, half: core * owned + (1 - half) * half_rows, other),
                (lambda core, half: (1 - core) * owned + half * half_rows, twin),
                (lambda core, half: (1 - core) * owned + (1 - half) * half_rows, grid.twin(other)),
            ]
            if step + 1 < grid.planes:
                ahead, parts = lax.optimization_barrier((above, parts))
        if step + 1 < grid.planes:
            held = ahead
            other = grid.along_y(held) if step % 2 else grid.along_x(held)
            twin = grid.twin(held)
            if step + 2 < grid.planes:
                above = grid.up(held)
        result = score(grid, step, pieces, ids, weights, parts, step == 0)
        parts = result
    rows = [row[None] for row in (values, rewards, ref_logprob, segment_end)]
    return finish(grid, parts, rows)


def solution(mesh):
    grid = Grid(mesh)
    placed = (
        P("batch", None),
        P("batch"),
        P(),
        P(None, ("batch", "vocab")),
        P(),
        P("batch"),
        P("batch"),
        P("batch"),
        P("batch"),
    )

    def body(*arrays):
        return per_device(grid, *arrays)

    return jax.shard_map(
        body,
        mesh=mesh,
        in_specs=placed,
        out_specs=(P("batch"), P("batch")),
        check_vma=False,
    )
```

time: 107 us -> 101 us (0.944)
  blocking collectives: 19.1 us -> 0 us
  starting transfers between devices: 11.1 us -> 20.8 us
  Pallas kernels: 54.9 us -> 58.1 us
  local copies, waits for them, and re-layouts: 2.79 us -> 0.03 us
  waiting for transfers between devices: 17.5 us -> 19.3 us
    all_to_all x2 -> x0, blocking collectives: 19.1 us -> none  [the longest x1 9.75 us: finish(): lax.all_to_all(heads, 'batch', split_axis=0, concat_axis=0, tiled=True)]
    ppermute x13 -> x20, starting transfers between devices: 11.1 us -> 20.8 us  [send(): return lax.ppermute(array, ('batch', 'vocab'), self.moves(target))]
    pallas_call x7 -> x9, Pallas kernels: 44.6 us -> 47.7 us  [the longest x4 39.3 us: score(): pl.pallas_call(lambda *refs: score_kernel(grid, step, offsets, first, *re...]
    unnamed x10 -> x12, local copies, waits for them, and re-layouts: 2.79 us -> 0.03 us
    ppermute x13 -> x20, waiting for transfers between devices: 17.5 us -> 19.3 us  [send(): return lax.ppermute(array, ('batch', 'vocab'), self.moves(target))]
  transfers between devices with their start and end apart: 13 -> 20, of which waited for: 7 -> 12; matrix products, arithmetic and copies ran while one was open for 0% -> 0% of each run, Pallas kernels for 38% -> 40%
where the time goes in v2:
time: 101 us; the launch traced here: 99.2 us
  Pallas kernels  58.1 us (58%)
  starting transfers between devices  20.8 us (21%)
  waiting for transfers between devices  19.3 us (19%)
    pallas_call x4, Pallas kernels, score(): pl.pallas_call(lambda *refs: score_kernel(grid, step, offsets, first, *re...  39.3 us
    ppermute x20, starting transfers between devices, send(): return lax.ppermute(array, ('batch', 'vocab'), self.moves(target))  20.8 us
    ppermute x20, waiting for transfers between devices, send(): return lax.ppermute(array, ('batch', 'vocab'), self.moves(target))  19.3 us
    pallas_call x1, Pallas kernels, per_device(): pl.pallas_call(load_kernel, out_shape=pltpu.VMEM(unembed.T.shape, unembed...  10.4 us
    pallas_call x2, Pallas kernels, normalize(): pl.pallas_call(lambda *refs: normalize_kernel(grid, halved, *refs), out_s...  6.83 us
  transfers between devices with their start and end apart: 20, of which 12 were waited for; matrix products, arithmetic and copies ran while one was open for 0% of the time, Pallas kernels for 40%

profile of v2, /device:TPU:1, one launch (start us, length us, event | category | flops | bytes accessed | tf_op | source)
XLA Modules:
  0.0 99.2 jit_solution(13103076836784161131)
XLA Ops:
  0.6 2.8 %share.1 = bf16[64,4096]{1,0:T(8,128)(2,1)} custom-call(bf16[128,4096]{1,0:T(8,128)(2,1)} %refs_0_.2, s32[1,128]{1,0:T(1,128)} %bitcast.18, f32[8,4096]{1,0:T(8,128)} %refs_2_.3), custom_call_target="tpu_custom_call" | custom-call | tf_op jit(solution)/shard_map/share/pallas_call | solution.py:127
  3.5 4.0 %normalize.1.refs_2_ = bf16[128,4096]{1,0:T(8,128)(2,1)} custom-call(bf16[128,4096]{1,0:T(8,128)(2,1)} %refs_0_.2, s32[1,128]{1,0:T(1,128)} %bitcast.19, f32[8,4096]{1,0:T(8,128)} %refs_2_.3), custom_call_target="tpu_custom_call" | custom-call | tf_op jit(solution)/shard_map/normalize/pallas_call | solution.py:127
  7.6 2.8 %collective-permute-start = (bf16[64,4096]{1,0:T(8,128)(2,1)}, bf16[64,4096]{1,0:T(8,128)(2,1)S(1)}, u32[]{:S(2)}, u32[]{:S(2)}) collective-permute-start(bf16[64,4096]{1,0:T(8,128)(2,1)} %share.1), channel_id=1, source_target_pairs={{0,8},{1,9},{2,10},{3,11},{4,12},{5,13},{6,14},{7,15},{8,24},{9,25... | collective-permute-start | bytes 1572872 | tf_op jit(solution)/shard_map/ppermute | solution.py:38
  10.3 10.4 %load.1.refs_1_ = bf16[4008,4096]{1,0:T(8,128)(2,1)S(1)} custom-call(bf16[4008,4096]{1,0:T(8,128)(2,1)} %bitcast.17), custom_call_target="tpu_custom_call" | custom-call | tf_op jit(solution)/shard_map/load/pallas_call | solution.py:402
  20.8 3.0 %collective-permute-done.refs_3_ = bf16[64,4096]{1,0:T(8,128)(2,1)S(1)} collective-permute-done((bf16[64,4096]{1,0:T(8,128)(2,1)}, bf16[64,4096]{1,0:T(8,128)(2,1)S(1)}, u32[]{:S(2)}, u32[]{:S(2)}) %collective-permute-start) | collective-permute-done | bytes 524320 | tf_op jit(solution)/shard_map/ppermute | solution.py:38
  24.4 1.3 %collective-permute-start.2 = (bf16[64,4096]{1,0:T(8,128)(2,1)S(1)}, bf16[64,4096]{1,0:T(8,128)(2,1)S(1)}, u32[]{:S(2)}, u32[]{:S(2)}) collective-permute-start(bf16[64,4096]{1,0:T(8,128)(2,1)S(1)} %collective-permute-done.refs_3_), channel_id=1, source_target_pairs={{0,1},{1,0},{2,3},{3,2},{4,5},{5,4},{6,7},{7,6},{8,9},{9,8},{10,11... | collective-permute-start | bytes 1572872 | tf_op jit(solution)/shard_map/ppermute | solution.py:38
  26.3 9.7 %shard_map.104.refs_2_ = f32[4,3,256]{2,1,0:T(4,128)S(1)} custom-call(s32[4,1,256]{2,1,0:T(1,128)S(1)} %bitcast.9, bf16[4008,4096]{1,0:T(8,128)(2,1)S(1)} %load.1.refs_1_, bf16[128,4096]{1,0:T(8,128)(2,1)S(1)} %copy-done, bf16[128,4096]{1,0:T(8,128)(2,1)S(1)} %collective-permute-done.3.refs_3_), custom_call_target="tpu_custom_call" | custom-call | flops 8405385216 | tf_op jit(solution)/shard_map/pallas_call | solution.py:228
  36.0 1.9 %collective-permute-done.2.refs_4_ = bf16[64,4096]{1,0:T(8,128)(2,1)S(1)} collective-permute-done((bf16[64,4096]{1,0:T(8,128)(2,1)S(1)}, bf16[64,4096]{1,0:T(8,128)(2,1)S(1)}, u32[]{:S(2)}, u32[]{:S(2)}) %collective-permute-start.2) | collective-permute-done | bytes 524320 | tf_op jit(solution)/shard_map/ppermute | solution.py:38
  37.9 0.9 collective-permute-start.7
  38.8 1.0 %collective-permute-done.1.refs_3_ = bf16[64,4096]{1,0:T(8,128)(2,1)S(1)} collective-permute-done((bf16[64,4096]{1,0:T(8,128)(2,1)S(1)}, bf16[64,4096]{1,0:T(8,128)(2,1)S(1)}, u32[]{:S(2)}, u32[]{:S(2)}) %collective-permute-start.1) | collective-permute-done | bytes 524320 | tf_op jit(solution)/shard_map/ppermute | solution.py:38
  39.8 1.1 %collective-permute-start.9 = (bf16[64,4096]{1,0:T(8,128)(2,1)S(1)}, bf16[64,4096]{1,0:T(8,128)(2,1)S(1)}, u32[]{:S(2)}, u32[]{:S(2)}) collective-permute-start(bf16[64,4096]{1,0:T(8,128)(2,1)S(1)} %collective-permute-done.1.refs_3_), channel_id=1, source_target_pairs={{0,4},{1,5},{2,6},{3,7},{4,0},{5,1},{6,2},{7,3},{8,12},{9,13},{10,... | collective-permute-start | bytes 1572872 | tf_op jit(solution)/shard_map/ppermute | solution.py:38
  40.9 1.2 %collective-permute-start.5 = (bf16[64,4096]{1,0:T(8,128)(2,1)S(1)}, bf16[64,4096]{1,0:T(8,128)(2,1)S(1)}, u32[]{:S(2)}, u32[]{:S(2)}) collective-permute-start(bf16[64,4096]{1,0:T(8,128)(2,1)S(1)} %collective-permute-done.1.refs_3_), channel_id=1, source_target_pairs={{0,2},{1,3},{2,0},{3,1},{4,6},{5,7},{6,4},{7,5},{8,10},{9,11},{10,... | collective-permute-start | bytes 1572872 | tf_op jit(solution)/shard_map/ppermute | solution.py:38
  42.7 9.7 %shard_map.105.refs_2_ = f32[4,3,256]{2,1,0:T(4,128)S(1)} custom-call(s32[4,1,256]{2,1,0:T(1,128)S(1)} %bitcast.10, bf16[4008,4096]{1,0:T(8,128)(2,1)S(1)} %load.1.refs_1_, f32[4,3,256]{2,1,0:T(4,128)S(1)} %shard_map.104.refs_2_, bf16[64,4096]{1,0:T(8,128)(2,1)S(1)} %collective-permute-done.refs_3_, bf16[64,4096]{1,0:T(8,128)(2,1)S(1)} %collective-permute-done.2.refs_4_, ...), custom_call_target="tpu_custom_call" | custom-call | flops 8405385216 | tf_op jit(solution)/shard_map/pallas_call | solution.py:228
  52.5 2.0 %collective-permute-done.5.refs_4_ = bf16[64,4096]{1,0:T(8,128)(2,1)S(1)} collective-permute-done((bf16[64,4096]{1,0:T(8,128)(2,1)S(1)}, bf16[64,4096]{1,0:T(8,128)(2,1)S(1)}, u32[]{:S(2)}, u32[]{:S(2)}) %collective-permute-start.5) | collective-permute-done | bytes 524320 | tf_op jit(solution)/shard_map/ppermute | solution.py:38
  54.4 0.9 collective-permute-start.10
  55.3 1.0 %collective-permute-done.4.refs_3_ = bf16[64,4096]{1,0:T(8,128)(2,1)S(1)} collective-permute-done((bf16[64,4096]{1,0:T(8,128)(2,1)S(1)}, bf16[64,4096]{1,0:T(8,128)(2,1)S(1)}, u32[]{:S(2)}, u32[]{:S(2)}) %collective-permute-start.4) | collective-permute-done | bytes 524320 | tf_op jit(solution)/shard_map/ppermute | solution.py:38
  56.3 1.1 %collective-permute-start.11 = (bf16[64,4096]{1,0:T(8,128)(2,1)S(1)}, bf16[64,4096]{1,0:T(8,128)(2,1)S(1)}, u32[]{:S(2)}, u32[]{:S(2)}) collective-permute-start(bf16[64,4096]{1,0:T(8,128)(2,1)S(1)} %collective-permute-done.4.refs_3_), channel_id=1, source_target_pairs={{0,4},{1,5},{2,6},{3,7},{4,0},{5,1},{6,2},{7,3},{8,12},{9,13},{10,... | collective-permute-start | bytes 1572872 | tf_op jit(solution)/shard_map/ppermute | solution.py:38
  57.7 9.9 %shard_map.106.refs_2_ = f32[4,3,256]{2,1,0:T(4,128)S(1)} custom-call(s32[4,1,256]{2,1,0:T(1,128)S(1)} %bitcast.11, bf16[4008,4096]{1,0:T(8,128)(2,1)S(1)} %load.1.refs_1_, f32[4,3,256]{2,1,0:T(4,128)S(1)} %shard_map.105.refs_2_, bf16[64,4096]{1,0:T(8,128)(2,1)S(1)} %collective-permute-done.1.refs_3_, bf16[64,4096]{1,0:T(8,128)(2,1)S(1)} %collective-permute-done.5.refs_4_, ...), custom_call_target="tpu_custom_call" | custom-call | flops 8405385216 | tf_op jit(solution)/shard_map/pallas_call | solution.py:228
  67.6 3.3 %collective-permute-done.8.refs_4_ = bf16[64,4096]{1,0:T(8,128)(2,1)S(1)} collective-permute-done((bf16[64,4096]{1,0:T(8,128)(2,1)S(1)}, bf16[64,4096]{1,0:T(8,128)(2,1)S(1)}, u32[]{:S(2)}, u32[]{:S(2)}) %collective-permute-start.8) | collective-permute-done | bytes 524320 | tf_op jit(solution)/shard_map/ppermute | solution.py:38
  70.9 0.9 collective-permute-start.12
  71.8 1.5 %collective-permute-done.12.refs_6_ = bf16[64,4096]{1,0:T(8,128)(2,1)S(1)} collective-permute-done((bf16[64,4096]{1,0:T(8,128)(2,1)S(1)}, bf16[64,4096]{1,0:T(8,128)(2,1)S(1)}, u32[]{:S(2)}, u32[]{:S(2)}) %collective-permute-start.12) | collective-permute-done | bytes 524320 | tf_op jit(solution)/shard_map/ppermute | solution.py:38
  73.3 10.0 %shard_map.107.refs_0_ = f32[4,3,256]{2,1,0:T(4,128)S(1)} custom-call(s32[4,1,256]{2,1,0:T(1,128)S(1)} %bitcast.12, bf16[4008,4096]{1,0:T(8,128)(2,1)S(1)} %load.1.refs_1_, f32[4,3,256]{2,1,0:T(4,128)S(1)} %shard_map.106.refs_2_, bf16[64,4096]{1,0:T(8,128)(2,1)S(1)} %collective-permute-done.4.refs_3_, bf16[64,4096]{1,0:T(8,128)(2,1)S(1)} %collective-permute-done.8.refs_4_, ...), custom_call_target="tpu_custom_call" | custom-call | flops 8405385216 | tf_op jit(solution)/shard_map/pallas_call | solution.py:228
  83.5 1.3 %collective-permute-start.14 = (f32[4,3,256]{2,1,0:T(4,128)S(1)}, f32[4,3,256]{2,1,0:T(4,128)S(1)}, u32[]{:S(2)}, u32[]{:S(2)}) collective-permute-start(f32[4,3,256]{2,1,0:T(4,128)S(1)} %shard_map.107.refs_0_), channel_id=1, source_target_pairs={{0,2},{1,3},{2,0},{3,1},{4,6},{5,7},{6,4},{7,5},{8,10},{9,11},{10,... | collective-permute-start | bytes 36872 | tf_op jit(solution)/shard_map/ppermute | solution.py:38
  84.8 1.2 %collective-permute-start.13 = (f32[4,3,256]{2,1,0:T(4,128)S(1)}, f32[4,3,256]{2,1,0:T(4,128)S(1)}, u32[]{:S(2)}, u32[]{:S(2)}) collective-permute-start(f32[4,3,256]{2,1,0:T(4,128)S(1)} %shard_map.107.refs_0_), channel_id=1, source_target_pairs={{0,1},{1,0},{2,3},{3,2},{4,5},{5,4},{6,7},{7,6},{8,9},{9,8},{10,11... | collective-permute-start | bytes 36872 | tf_op jit(solution)/shard_map/ppermute | solution.py:38
  86.0 0.8 collective-permute-done.15.refs_3_
  87.9 1.9 %collective-permute-start.16 = (f32[16,256]{1,0:T(8,128)S(1)}, f32[16,256]{1,0:T(8,128)S(1)}, u32[]{:S(2)}, u32[]{:S(2)}) collective-permute-start(f32[16,256]{1,0:T(8,128)S(1)} %shard_map.108.refs_0_), channel_id=1, source_target_pairs={{0,4},{1,5},{2,6},{3,7},{4,0},{5,1},{6,2},{7,3},{8,12},{9,13},{10,... | collective-permute-start | bytes 49160 | tf_op jit(solution)/shard_map/ppermute | solution.py:38
  89.7 0.8 collective-permute-done.16.refs_1_
  90.6 1.3 %collective-permute-start.19 = (f32[16,256]{1,0:T(8,128)S(1)}, f32[16,256]{1,0:T(8,128)S(1)}, u32[]{:S(2)}, u32[]{:S(2)}) collective-permute-start(f32[16,256]{1,0:T(8,128)S(1)} %shard_map.109.refs_0_), channel_id=1, source_target_pairs={{0,16},{1,17},{2,18},{3,19},{4,20},{5,21},{6,22},{7,23},{8,0},{9,1... | collective-permute-start | bytes 49160 | tf_op jit(solution)/shard_map/ppermute | solution.py:38
  91.9 2.2 %collective-permute-start.18 = (f32[16,256]{1,0:T(8,128)S(1)}, f32[16,256]{1,0:T(8,128)S(1)}, u32[]{:S(2)}, u32[]{:S(2)}) collective-permute-start(f32[16,256]{1,0:T(8,128)S(1)} %shard_map.109.refs_0_), channel_id=1, source_target_pairs={{0,24},{1,25},{2,26},{3,27},{4,28},{5,29},{6,30},{7,31},{8,16},{9,... | collective-permute-start | bytes 49160 | tf_op jit(solution)/shard_map/ppermute | solution.py:38
  94.6 1.8 %collective-permute-done.18.refs_2_ = f32[16,256]{1,0:T(8,128)S(1)} collective-permute-done((f32[16,256]{1,0:T(8,128)S(1)}, f32[16,256]{1,0:T(8,128)S(1)}, u32[]{:S(2)}, u32[]{:S(2)}) %collective-permute-start.18) | collective-permute-done | bytes 16416 | tf_op jit(solution)/shard_map/ppermute | solution.py:38
  96.4 1.3 %collective-permute-done.17.refs_1_ = f32[16,256]{1,0:T(8,128)S(1)} collective-permute-done((f32[16,256]{1,0:T(8,128)S(1)}, f32[16,256]{1,0:T(8,128)S(1)}, u32[]{:S(2)}, u32[]{:S(2)}) %collective-permute-start.17) | collective-permute-done | bytes 16416 | tf_op jit(solution)/shard_map/ppermute | solution.py:38
  97.7 1.3 %shard_map.110 = (f32[1,128]{1,0:T(1,128)}, f32[1,128]{1,0:T(1,128)}) custom-call(f32[16,256]{1,0:T(8,128)S(1)} %shard_map.109.refs_0_, f32[16,256]{1,0:T(8,128)S(1)} %collective-permute-done.17.refs_1_, f32[16,256]{1,0:T(8,128)S(1)} %collective-permute-done.18.refs_2_, f32[16,256]{1,0:T(8,128)S(1)} %collective-permute-done.19.refs_3_), custom_call_target="tpu_custom_call" | custom-call | tf_op jit(solution)/shard_map/pallas_call | solution.py:278
  (30 shorter events, 3.9 us)
Async XLA Ops:
  7.5 18.8 %collective-permute-start.3 = (bf16[128,4096]{1,0:T(8,128)(2,1)}, bf16[128,4096]{1,0:T(8,128)(2,1)S(1)}, u32[]{:S(2)}, u32[]{:S(2)}) collective-permute-start(bf16[128,4096]{1,0:T(8,128)(2,1)} %normalize.1.refs_2_), channel_id=1, source_target_pairs={{0,4},{1,5},{2,6},{3,7},{4,0},{5,1},{6,2},{7,3},{8,12},{9,13},{10,... | collective-permute-start | bytes 3145736 | tf_op jit(solution)/shard_map/ppermute | solution.py:38
  7.6 16.2 %collective-permute-start = (bf16[64,4096]{1,0:T(8,128)(2,1)}, bf16[64,4096]{1,0:T(8,128)(2,1)S(1)}, u32[]{:S(2)}, u32[]{:S(2)}) collective-permute-start(bf16[64,4096]{1,0:T(8,128)(2,1)} %share.1), channel_id=1, source_target_pairs={{0,8},{1,9},{2,10},{3,11},{4,12},{5,13},{6,14},{7,15},{8,24},{9,25... | collective-permute-start | bytes 1572872 | tf_op jit(solution)/shard_map/ppermute | solution.py:38
  10.3 16.0 %copy-start = (bf16[128,4096]{1,0:T(8,128)(2,1)S(1)}, bf16[128,4096]{1,0:T(8,128)(2,1)}, u32[]{:S(2)}) copy-start(bf16[128,4096]{1,0:T(8,128)(2,1)} %normalize.1.refs_2_) | copy-start | bytes 3145732
  10.3 16.0 %copy-start.1 = (s32[1024]{0:T(1024)S(1)}, s32[1024]{0:T(1024)}, u32[]{:S(2)}) copy-start(s32[1024]{0:T(1024)} %param.13) | copy-start | bytes 12292
  23.8 18.9 %collective-permute-start.6 = (bf16[64,4096]{1,0:T(8,128)(2,1)S(1)}, bf16[64,4096]{1,0:T(8,128)(2,1)S(1)}, u32[]{:S(2)}, u32[]{:S(2)}) collective-permute-start(bf16[64,4096]{1,0:T(8,128)(2,1)S(1)} %collective-permute-done.refs_3_), channel_id=1, source_target_pairs={{0,4},{1,5},{2,6},{3,7},{4,0},{5,1},{6,2},{7,3},{8,12},{9,13},{10,... | collective-permute-start | bytes 1572872 | tf_op jit(solution)/shard_map/ppermute | solution.py:38
  24.4 13.5 %collective-permute-start.2 = (bf16[64,4096]{1,0:T(8,128)(2,1)S(1)}, bf16[64,4096]{1,0:T(8,128)(2,1)S(1)}, u32[]{:S(2)}, u32[]{:S(2)}) collective-permute-start(bf16[64,4096]{1,0:T(8,128)(2,1)S(1)} %collective-permute-done.refs_3_), channel_id=1, source_target_pairs={{0,1},{1,0},{2,3},{3,2},{4,5},{5,4},{6,7},{7,6},{8,9},{9,8},{10,11... | collective-permute-start | bytes 1572872 | tf_op jit(solution)/shard_map/ppermute | solution.py:38
  25.7 14.1 %collective-permute-start.1 = (bf16[64,4096]{1,0:T(8,128)(2,1)S(1)}, bf16[64,4096]{1,0:T(8,128)(2,1)S(1)}, u32[]{:S(2)}, u32[]{:S(2)}) collective-permute-start(bf16[64,4096]{1,0:T(8,128)(2,1)S(1)} %collective-permute-done.refs_3_), channel_id=1, source_target_pairs={{0,8},{1,9},{2,10},{3,11},{4,12},{5,13},{6,14},{7,15},{8,24},{9,25... | collective-permute-start | bytes 1572872 | tf_op jit(solution)/shard_map/ppermute | solution.py:38
  37.9 4.8 %collective-permute-start.7 = (bf16[64,4096]{1,0:T(8,128)(2,1)S(1)}, bf16[64,4096]{1,0:T(8,128)(2,1)S(1)}, u32[]{:S(2)}, u32[]{:S(2)}) collective-permute-start(bf16[64,4096]{1,0:T(8,128)(2,1)S(1)} %collective-permute-done.2.refs_4_), channel_id=1, source_target_pairs={{0,4},{1,5},{2,6},{3,7},{4,0},{5,1},{6,2},{7,3},{8,12},{9,13},{10,... | collective-permute-start | bytes 1572872 | tf_op jit(solution)/shard_map/ppermute | solution.py:38
  39.8 17.9 %collective-permute-start.9 = (bf16[64,4096]{1,0:T(8,128)(2,1)S(1)}, bf16[64,4096]{1,0:T(8,128)(2,1)S(1)}, u32[]{:S(2)}, u32[]{:S(2)}) collective-permute-start(bf16[64,4096]{1,0:T(8,128)(2,1)S(1)} %collective-permute-done.1.refs_3_), channel_id=1, source_target_pairs={{0,4},{1,5},{2,6},{3,7},{4,0},{5,1},{6,2},{7,3},{8,12},{9,13},{10,... | collective-permute-start | bytes 1572872 | tf_op jit(solution)/shard_map/ppermute | solution.py:38
  40.9 13.5 %collective-permute-start.5 = (bf16[64,4096]{1,0:T(8,128)(2,1)S(1)}, bf16[64,4096]{1,0:T(8,128)(2,1)S(1)}, u32[]{:S(2)}, u32[]{:S(2)}) collective-permute-start(bf16[64,4096]{1,0:T(8,128)(2,1)S(1)} %collective-permute-done.1.refs_3_), channel_id=1, source_target_pairs={{0,2},{1,3},{2,0},{3,1},{4,6},{5,7},{6,4},{7,5},{8,10},{9,11},{10,... | collective-permute-start | bytes 1572872 | tf_op jit(solution)/shard_map/ppermute | solution.py:38
  42.2 14.1 %collective-permute-start.4 = (bf16[64,4096]{1,0:T(8,128)(2,1)S(1)}, bf16[64,4096]{1,0:T(8,128)(2,1)S(1)}, u32[]{:S(2)}, u32[]{:S(2)}) collective-permute-start(bf16[64,4096]{1,0:T(8,128)(2,1)S(1)} %collective-permute-done.1.refs_3_), channel_id=1, source_target_pairs={{0,8},{1,9},{2,10},{3,11},{4,12},{5,13},{6,14},{7,15},{8,24},{9,25... | collective-permute-start | bytes 1572872 | tf_op jit(solution)/shard_map/ppermute | solution.py:38
  52.4 35.3 %copy-start.2 = (f32[128]{0:T(128)S(1)}, f32[128]{0:T(128)}, u32[]{:S(2)}) copy-start(f32[128]{0:T(128)} %param.14) | copy-start | bytes 1540
  52.4 35.2 %copy-start.3 = (f32[128]{0:T(128)S(1)}, f32[128]{0:T(128)}, u32[]{:S(2)}) copy-start(f32[128]{0:T(128)} %param.15) | copy-start | bytes 1540
  52.4 35.2 %copy-start.4 = (f32[128]{0:T(128)S(1)}, f32[128]{0:T(128)}, u32[]{:S(2)}) copy-start(f32[128]{0:T(128)} %param.16) | copy-start | bytes 1540
  52.4 35.2 %copy-start.5 = (s32[128]{0:T(128)S(1)}, s32[128]{0:T(128)}, u32[]{:S(2)}) copy-start(s32[128]{0:T(128)} %param.17) | copy-start | bytes 1540
  54.4 3.3 %collective-permute-start.10 = (bf16[64,4096]{1,0:T(8,128)(2,1)S(1)}, bf16[64,4096]{1,0:T(8,128)(2,1)S(1)}, u32[]{:S(2)}, u32[]{:S(2)}) collective-permute-start(bf16[64,4096]{1,0:T(8,128)(2,1)S(1)} %collective-permute-done.5.refs_4_), channel_id=1, source_target_pairs={{0,4},{1,5},{2,6},{3,7},{4,0},{5,1},{6,2},{7,3},{8,12},{9,13},{10,... | collective-permute-start | bytes 1572872 | tf_op jit(solution)/shard_map/ppermute | solution.py:38
  56.3 15.5 %collective-permute-start.11 = (bf16[64,4096]{1,0:T(8,128)(2,1)S(1)}, bf16[64,4096]{1,0:T(8,128)(2,1)S(1)}, u32[]{:S(2)}, u32[]{:S(2)}) collective-permute-start(bf16[64,4096]{1,0:T(8,128)(2,1)S(1)} %collective-permute-done.4.refs_3_), channel_id=1, source_target_pairs={{0,4},{1,5},{2,6},{3,7},{4,0},{5,1},{6,2},{7,3},{8,12},{9,13},{10,... | collective-permute-start | bytes 1572872 | tf_op jit(solution)/shard_map/ppermute | solution.py:38
  57.4 13.5 %collective-permute-start.8 = (bf16[64,4096]{1,0:T(8,128)(2,1)S(1)}, bf16[64,4096]{1,0:T(8,128)(2,1)S(1)}, u32[]{:S(2)}, u32[]{:S(2)}) collective-permute-start(bf16[64,4096]{1,0:T(8,128)(2,1)S(1)} %collective-permute-done.4.refs_3_), channel_id=1, source_target_pairs={{0,1},{1,0},{2,3},{3,2},{4,5},{5,4},{6,7},{7,6},{8,9},{9,8},{10,11... | collective-permute-start | bytes 1572872 | tf_op jit(solution)/shard_map/ppermute | solution.py:38
  70.9 2.4 %collective-permute-start.12 = (bf16[64,4096]{1,0:T(8,128)(2,1)S(1)}, bf16[64,4096]{1,0:T(8,128)(2,1)S(1)}, u32[]{:S(2)}, u32[]{:S(2)}) collective-permute-start(bf16[64,4096]{1,0:T(8,128)(2,1)S(1)} %collective-permute-done.8.refs_4_), channel_id=1, source_target_pairs={{0,4},{1,5},{2,6},{3,7},{4,0},{5,1},{6,2},{7,3},{8,12},{9,13},{10,... | collective-permute-start | bytes 1572872 | tf_op jit(solution)/shard_map/ppermute | solution.py:38
  83.3 3.6 %collective-permute-start.15 = (f32[4,3,256]{2,1,0:T(4,128)S(1)}, f32[4,3,256]{2,1,0:T(4,128)S(1)}, u32[]{:S(2)}, u32[]{:S(2)}) collective-permute-start(f32[4,3,256]{2,1,0:T(4,128)S(1)} %shard_map.107.refs_0_), channel_id=1, source_target_pairs={{0,3},{1,2},{2,1},{3,0},{4,7},{5,6},{6,5},{7,4},{8,11},{9,10},{10,... | collective-permute-start | bytes 36872 | tf_op jit(solution)/shard_map/ppermute | solution.py:38
  83.5 3.3 %collective-permute-start.14 = (f32[4,3,256]{2,1,0:T(4,128)S(1)}, f32[4,3,256]{2,1,0:T(4,128)S(1)}, u32[]{:S(2)}, u32[]{:S(2)}) collective-permute-start(f32[4,3,256]{2,1,0:T(4,128)S(1)} %shard_map.107.refs_0_), channel_id=1, source_target_pairs={{0,2},{1,3},{2,0},{3,1},{4,6},{5,7},{6,4},{7,5},{8,10},{9,11},{10,... | collective-permute-start | bytes 36872 | tf_op jit(solution)/shard_map/ppermute | solution.py:38
  84.8 2.9 %collective-permute-start.13 = (f32[4,3,256]{2,1,0:T(4,128)S(1)}, f32[4,3,256]{2,1,0:T(4,128)S(1)}, u32[]{:S(2)}, u32[]{:S(2)}) collective-permute-start(f32[4,3,256]{2,1,0:T(4,128)S(1)} %shard_map.107.refs_0_), channel_id=1, source_target_pairs={{0,1},{1,0},{2,3},{3,2},{4,5},{5,4},{6,7},{7,6},{8,9},{9,8},{10,11... | collective-permute-start | bytes 36872 | tf_op jit(solution)/shard_map/ppermute | solution.py:38
  87.9 2.7 %collective-permute-start.16 = (f32[16,256]{1,0:T(8,128)S(1)}, f32[16,256]{1,0:T(8,128)S(1)}, u32[]{:S(2)}, u32[]{:S(2)}) collective-permute-start(f32[16,256]{1,0:T(8,128)S(1)} %shard_map.108.refs_0_), channel_id=1, source_target_pairs={{0,4},{1,5},{2,6},{3,7},{4,0},{5,1},{6,2},{7,3},{8,12},{9,13},{10,... | collective-permute-start | bytes 49160 | tf_op jit(solution)/shard_map/ppermute | solution.py:38
  90.6 3.9 %collective-permute-start.19 = (f32[16,256]{1,0:T(8,128)S(1)}, f32[16,256]{1,0:T(8,128)S(1)}, u32[]{:S(2)}, u32[]{:S(2)}) collective-permute-start(f32[16,256]{1,0:T(8,128)S(1)} %shard_map.109.refs_0_), channel_id=1, source_target_pairs={{0,16},{1,17},{2,18},{3,19},{4,20},{5,21},{6,22},{7,23},{8,0},{9,1... | collective-permute-start | bytes 49160 | tf_op jit(solution)/shard_map/ppermute | solution.py:38
  91.9 4.5 %collective-permute-start.18 = (f32[16,256]{1,0:T(8,128)S(1)}, f32[16,256]{1,0:T(8,128)S(1)}, u32[]{:S(2)}, u32[]{:S(2)}) collective-permute-start(f32[16,256]{1,0:T(8,128)S(1)} %shard_map.109.refs_0_), channel_id=1, source_target_pairs={{0,24},{1,25},{2,26},{3,27},{4,28},{5,29},{6,30},{7,31},{8,16},{9,... | collective-permute-start | bytes 49160 | tf_op jit(solution)/shard_map/ppermute | solution.py:38
  94.1 3.6 %collective-permute-start.17 = (f32[16,256]{1,0:T(8,128)S(1)}, f32[16,256]{1,0:T(8,128)S(1)}, u32[]{:S(2)}, u32[]{:S(2)}) collective-permute-start(f32[16,256]{1,0:T(8,128)S(1)} %shard_map.109.refs_0_), channel_id=1, source_target_pairs={{0,8},{1,9},{2,10},{3,11},{4,12},{5,13},{6,14},{7,15},{8,24},{9,25... | collective-permute-start | bytes 49160 | tf_op jit(solution)/shard_map/ppermute | solution.py:38

commit v3 on v2

--- a/solution.py
+++ b/solution.py
@@ -80,7 +80,8 @@
     block = 16
     chunk = 32
     exits = gains_ref.shape[0]
-    start = pl.multiple_of(grid.place()[2] * rows, rows) if halved else 0
+    half = grid.place()[2]
+    start = pl.multiple_of((half if halved else 1 - half) * rows, rows)
     small = [
         pltpu.make_async_copy(layers_hbm, layers_ref, sem.at[0]),
         pltpu.make_async_copy(gains_hbm, gains_ref, sem.at[1]),
@@ -123,7 +124,7 @@
 
 def normalize(grid, halved, hidden, layers, gains):
     owned, width = hidden.shape
-    rows = owned // 2 if halved else owned
+    rows = owned // 2
     return pl.pallas_call(
         lambda *refs: normalize_kernel(grid, halved, *refs),
         out_shape=jax.ShapeDtypeStruct((rows, width), jnp.bfloat16),
@@ -206,7 +207,7 @@
 
 
 def score(grid, step, pieces, ids, weights, parts, first):
-    owned = pieces[0][1].shape[0] if first else pieces[0][1].shape[0] * 2
+    owned = pieces[0][1].shape[0] * 2
     width = weights.shape[1]
     rows = weights.shape[0]
     tokens = owned * CORES
@@ -409,14 +410,16 @@
         name="load",
     )(unembed.T)
     parts = None
-    twin = grid.twin(normed)
+    twin = grid.twin(held)
     above = grid.up(held)
     other = None
     for step in range(grid.planes):
         if step == 0:
             pieces = [
-                (lambda core, half: core * owned, normed),
-                (lambda core, half: (1 - core) * owned, twin),
+                (lambda core, half: core * owned + half * half_rows, held),
+                (lambda core, half: core * owned + (1 - half) * half_rows, normed),
+                (lambda core, half: (1 - core) * owned + half * half_rows, twin),
+                (lambda core, half: (1 - core) * owned + (1 - half) * half_rows, grid.twin(normed)),
             ]
             ahead, weights = lax.optimization_barrier((above, weights))
         else:

time: 101 us -> 96.5 us (0.955)
  the two profiles are of different devices: /device:TPU:1 before, /device:TPU:0 now
where the time goes in v3:
time: 96.5 us; the launch traced here: 96.4 us
  Pallas kernels  57 us (59%)
  starting transfers between devices  19.3 us (20%)
  waiting for transfers between devices  19 us (20%)
  between operations  1.01 us (1%)
    pallas_call x4, Pallas kernels, score(): pl.pallas_call(lambda *refs: score_kernel(grid, step, offsets, first, *re...  39.4 us
    ppermute x21, starting transfers between devices, send(): return lax.ppermute(array, ('batch', 'vocab'), self.moves(target))  19.3 us
    ppermute x21, waiting for transfers between devices, send(): return lax.ppermute(array, ('batch', 'vocab'), self.moves(target))  19 us
    pallas_call x1, Pallas kernels, per_device(): pl.pallas_call(load_kernel, out_shape=pltpu.VMEM(unembed.T.shape, unembed...  10.4 us
    pallas_call x2, Pallas kernels, normalize(): pl.pallas_call(lambda *refs: normalize_kernel(grid, halved, *refs), out_s...  5.65 us
  transfers between devices with their start and end apart: 21, of which 11 were waited for; matrix products, arithmetic and copies ran while one was open for 0% of the time, Pallas kernels for 44%

profile of v3, /device:TPU:0, one launch (start us, length us, event | category | flops | bytes accessed | tf_op | source)
XLA Modules:
  0.0 96.4 jit_solution(8408990882268202128)
XLA Ops:
  0.6 2.8 %share.1.refs_2_ = bf16[64,4096]{1,0:T(8,128)(2,1)} custom-call(bf16[128,4096]{1,0:T(8,128)(2,1)} %refs_0_.2, s32[1,128]{1,0:T(1,128)} %bitcast.18, f32[8,4096]{1,0:T(8,128)} %refs_2_.3), custom_call_target="tpu_custom_call" | custom-call | tf_op jit(solution)/shard_map/share/pallas_call | solution.py:128
  3.5 3.1 %collective-permute-start = (bf16[64,4096]{1,0:T(8,128)(2,1)}, bf16[64,4096]{1,0:T(8,128)(2,1)S(1)}, u32[]{:S(2)}, u32[]{:S(2)}) collective-permute-start(bf16[64,4096]{1,0:T(8,128)(2,1)} %share.1.refs_2_), channel_id=1, source_target_pairs={{0,8},{1,9},{2,10},{3,11},{4,12},{5,13},{6,14},{7,15},{8,24},{9,25... | collective-permute-start | bytes 1572872 | tf_op jit(solution)/shard_map/ppermute | solution.py:38
  6.6 2.8 %normalize.1.refs_3_ = bf16[64,4096]{1,0:T(8,128)(2,1)} custom-call(bf16[128,4096]{1,0:T(8,128)(2,1)} %refs_0_.2, s32[1,128]{1,0:T(1,128)} %bitcast.19, f32[8,4096]{1,0:T(8,128)} %refs_2_.3), custom_call_target="tpu_custom_call" | custom-call | tf_op jit(solution)/shard_map/normalize/pallas_call | solution.py:128
  9.5 0.5 collective-permute-start.3
  10.0 10.4 %load.1.refs_1_ = bf16[4008,4096]{1,0:T(8,128)(2,1)S(1)} custom-call(bf16[4008,4096]{1,0:T(8,128)(2,1)} %bitcast.17), custom_call_target="tpu_custom_call" | custom-call | tf_op jit(solution)/shard_map/load/pallas_call | solution.py:403
  20.6 1.5 %collective-permute-start.2 = (bf16[64,4096]{1,0:T(8,128)(2,1)S(1)}, bf16[64,4096]{1,0:T(8,128)(2,1)S(1)}, u32[]{:S(2)}, u32[]{:S(2)}) collective-permute-start(bf16[64,4096]{1,0:T(8,128)(2,1)S(1)} %collective-permute-done.refs_3_), channel_id=1, source_target_pairs={{0,1},{1,0},{2,3},{3,2},{4,5},{5,4},{6,7},{7,6},{8,9},{9,8},{10,11... | collective-permute-start | bytes 1572872 | tf_op jit(solution)/shard_map/ppermute | solution.py:38
  22.1 2.6 %collective-permute-start.1 = (bf16[64,4096]{1,0:T(8,128)(2,1)S(1)}, bf16[64,4096]{1,0:T(8,128)(2,1)S(1)}, u32[]{:S(2)}, u32[]{:S(2)}) collective-permute-start(bf16[64,4096]{1,0:T(8,128)(2,1)S(1)} %collective-permute-done.refs_3_), channel_id=1, source_target_pairs={{0,8},{1,9},{2,10},{3,11},{4,12},{5,13},{6,14},{7,15},{8,24},{9,25... | collective-permute-start | bytes 1572872 | tf_op jit(solution)/shard_map/ppermute | solution.py:38
  24.7 9.7 %shard_map.104.refs_2_ = f32[4,3,256]{2,1,0:T(4,128)S(1)} custom-call(s32[4,1,256]{2,1,0:T(1,128)S(1)} %bitcast.9, bf16[4008,4096]{1,0:T(8,128)(2,1)S(1)} %load.1.refs_1_, bf16[64,4096]{1,0:T(8,128)(2,1)S(1)} %copy-done, bf16[64,4096]{1,0:T(8,128)(2,1)S(1)} %copy-done.1, bf16[64,4096]{1,0:T(8,128)(2,1)S(1)} %collective-permute-done.3.refs_4_, ...), custom_call_target="tpu_custom_call" | custom-call | flops 8405385216 | tf_op jit(solution)/shard_map/pallas_call | solution.py:229
  34.4 0.4 collective-permute-done.2.refs_4_
  34.8 2.1 %collective-permute-done.1.refs_3_ = bf16[64,4096]{1,0:T(8,128)(2,1)S(1)} collective-permute-done((bf16[64,4096]{1,0:T(8,128)(2,1)S(1)}, bf16[64,4096]{1,0:T(8,128)(2,1)S(1)}, u32[]{:S(2)}, u32[]{:S(2)}) %collective-permute-start.1) | collective-permute-done | bytes 524320 | tf_op jit(solution)/shard_map/ppermute | solution.py:38
  37.0 1.5 %collective-permute-start.6 = (bf16[64,4096]{1,0:T(8,128)(2,1)S(1)}, bf16[64,4096]{1,0:T(8,128)(2,1)S(1)}, u32[]{:S(2)}, u32[]{:S(2)}) collective-permute-start(bf16[64,4096]{1,0:T(8,128)(2,1)S(1)} %collective-permute-done.1.refs_3_), channel_id=1, source_target_pairs={{0,2},{1,3},{2,0},{3,1},{4,6},{5,7},{6,4},{7,5},{8,10},{9,11},{10,... | collective-permute-start | bytes 1572872 | tf_op jit(solution)/shard_map/ppermute | solution.py:38
  38.5 1.7 %collective-permute-start.5 = (bf16[64,4096]{1,0:T(8,128)(2,1)S(1)}, bf16[64,4096]{1,0:T(8,128)(2,1)S(1)}, u32[]{:S(2)}, u32[]{:S(2)}) collective-permute-start(bf16[64,4096]{1,0:T(8,128)(2,1)S(1)} %collective-permute-done.1.refs_3_), channel_id=1, source_target_pairs={{0,8},{1,9},{2,10},{3,11},{4,12},{5,13},{6,14},{7,15},{8,24},{9,25... | collective-permute-start | bytes 1572872 | tf_op jit(solution)/shard_map/ppermute | solution.py:38
  40.2 9.7 %shard_map.105.refs_2_ = f32[4,3,256]{2,1,0:T(4,128)S(1)} custom-call(s32[4,1,256]{2,1,0:T(1,128)S(1)} %bitcast.10, bf16[4008,4096]{1,0:T(8,128)(2,1)S(1)} %load.1.refs_1_, f32[4,3,256]{2,1,0:T(4,128)S(1)} %shard_map.104.refs_2_, bf16[64,4096]{1,0:T(8,128)(2,1)S(1)} %collective-permute-done.refs_3_, bf16[64,4096]{1,0:T(8,128)(2,1)S(1)} %collective-permute-done.2.refs_4_, ...), custom_call_target="tpu_custom_call" | custom-call | flops 8405385216 | tf_op jit(solution)/shard_map/pallas_call | solution.py:229
  49.9 1.4 %collective-permute-done.6.refs_4_ = bf16[64,4096]{1,0:T(8,128)(2,1)S(1)} collective-permute-done((bf16[64,4096]{1,0:T(8,128)(2,1)S(1)}, bf16[64,4096]{1,0:T(8,128)(2,1)S(1)}, u32[]{:S(2)}, u32[]{:S(2)}) %collective-permute-start.6) | collective-permute-done | bytes 524320 | tf_op jit(solution)/shard_map/ppermute | solution.py:38
  51.3 2.1 %collective-permute-done.5.refs_3_ = bf16[64,4096]{1,0:T(8,128)(2,1)S(1)} collective-permute-done((bf16[64,4096]{1,0:T(8,128)(2,1)S(1)}, bf16[64,4096]{1,0:T(8,128)(2,1)S(1)}, u32[]{:S(2)}, u32[]{:S(2)}) %collective-permute-start.5) | collective-permute-done | bytes 524320 | tf_op jit(solution)/shard_map/ppermute | solution.py:38
  53.4 0.5 collective-permute-start.9
  54.0 9.9 %shard_map.106.refs_2_ = f32[4,3,256]{2,1,0:T(4,128)S(1)} custom-call(s32[4,1,256]{2,1,0:T(1,128)S(1)} %bitcast.11, bf16[4008,4096]{1,0:T(8,128)(2,1)S(1)} %load.1.refs_1_, f32[4,3,256]{2,1,0:T(4,128)S(1)} %shard_map.105.refs_2_, bf16[64,4096]{1,0:T(8,128)(2,1)S(1)} %collective-permute-done.1.refs_3_, bf16[64,4096]{1,0:T(8,128)(2,1)S(1)} %collective-permute-done.6.refs_4_, ...), custom_call_target="tpu_custom_call" | custom-call | flops 8405385216 | tf_op jit(solution)/shard_map/pallas_call | solution.py:229
  63.9 3.9 %collective-permute-done.9.refs_4_ = bf16[64,4096]{1,0:T(8,128)(2,1)S(1)} collective-permute-done((bf16[64,4096]{1,0:T(8,128)(2,1)S(1)}, bf16[64,4096]{1,0:T(8,128)(2,1)S(1)}, u32[]{:S(2)}, u32[]{:S(2)}) %collective-permute-start.9) | collective-permute-done | bytes 524320 | tf_op jit(solution)/shard_map/ppermute | solution.py:38
  67.8 1.9 %collective-permute-done.13.refs_6_ = bf16[64,4096]{1,0:T(8,128)(2,1)S(1)} collective-permute-done((bf16[64,4096]{1,0:T(8,128)(2,1)S(1)}, bf16[64,4096]{1,0:T(8,128)(2,1)S(1)}, u32[]{:S(2)}, u32[]{:S(2)}) %collective-permute-start.13) | collective-permute-done | bytes 524320 | tf_op jit(solution)/shard_map/ppermute | solution.py:38
  69.7 10.0 %shard_map.107.refs_0_ = f32[4,3,256]{2,1,0:T(4,128)S(1)} custom-call(s32[4,1,256]{2,1,0:T(1,128)S(1)} %bitcast.12, bf16[4008,4096]{1,0:T(8,128)(2,1)S(1)} %load.1.refs_1_, f32[4,3,256]{2,1,0:T(4,128)S(1)} %shard_map.106.refs_2_, bf16[64,4096]{1,0:T(8,128)(2,1)S(1)} %collective-permute-done.5.refs_3_, bf16[64,4096]{1,0:T(8,128)(2,1)S(1)} %collective-permute-done.9.refs_4_, ...), custom_call_target="tpu_custom_call" | custom-call | flops 8405385216 | tf_op jit(solution)/shard_map/pallas_call | solution.py:229
  79.7 0.5 collective-permute-start.16
  80.2 1.5 %collective-permute-start.15 = (f32[4,3,256]{2,1,0:T(4,128)S(1)}, f32[4,3,256]{2,1,0:T(4,128)S(1)}, u32[]{:S(2)}, u32[]{:S(2)}) collective-permute-start(f32[4,3,256]{2,1,0:T(4,128)S(1)} %shard_map.107.refs_0_), channel_id=1, source_target_pairs={{0,2},{1,3},{2,0},{3,1},{4,6},{5,7},{6,4},{7,5},{8,10},{9,11},{10,... | collective-permute-start | bytes 36872 | tf_op jit(solution)/shard_map/ppermute | solution.py:38
  81.7 1.5 %collective-permute-start.14 = (f32[4,3,256]{2,1,0:T(4,128)S(1)}, f32[4,3,256]{2,1,0:T(4,128)S(1)}, u32[]{:S(2)}, u32[]{:S(2)}) collective-permute-start(f32[4,3,256]{2,1,0:T(4,128)S(1)} %shard_map.107.refs_0_), channel_id=1, source_target_pairs={{0,1},{1,0},{2,3},{3,2},{4,5},{5,4},{6,7},{7,6},{8,9},{9,8},{10,11... | collective-permute-start | bytes 36872 | tf_op jit(solution)/shard_map/ppermute | solution.py:38
  83.2 1.1 %collective-permute-done.16.refs_3_ = f32[4,3,256]{2,1,0:T(4,128)S(1)} collective-permute-done((f32[4,3,256]{2,1,0:T(4,128)S(1)}, f32[4,3,256]{2,1,0:T(4,128)S(1)}, u32[]{:S(2)}, u32[]{:S(2)}) %collective-permute-start.16) | collective-permute-done | bytes 12320 | tf_op jit(solution)/shard_map/ppermute | solution.py:38
  84.4 1.1 %collective-permute-done.14.refs_1_ = f32[4,3,256]{2,1,0:T(4,128)S(1)} collective-permute-done((f32[4,3,256]{2,1,0:T(4,128)S(1)}, f32[4,3,256]{2,1,0:T(4,128)S(1)}, u32[]{:S(2)}, u32[]{:S(2)}) %collective-permute-start.14) | collective-permute-done | bytes 12320 | tf_op jit(solution)/shard_map/ppermute | solution.py:38
  85.8 1.2 %collective-permute-done.17.refs_1_ = f32[16,256]{1,0:T(8,128)S(1)} collective-permute-done((f32[16,256]{1,0:T(8,128)S(1)}, f32[16,256]{1,0:T(8,128)S(1)}, u32[]{:S(2)}, u32[]{:S(2)}) %collective-permute-start.17) | collective-permute-done | bytes 16416 | tf_op jit(solution)/shard_map/ppermute | solution.py:38
  87.0 0.8 collective-permute-start.20
  87.8 2.4 %collective-permute-start.19 = (f32[16,256]{1,0:T(8,128)S(1)}, f32[16,256]{1,0:T(8,128)S(1)}, u32[]{:S(2)}, u32[]{:S(2)}) collective-permute-start(f32[16,256]{1,0:T(8,128)S(1)} %shard_map.109.refs_0_), channel_id=1, source_target_pairs={{0,24},{1,25},{2,26},{3,27},{4,28},{5,29},{6,30},{7,31},{8,16},{9,... | collective-permute-start | bytes 49160 | tf_op jit(solution)/shard_map/ppermute | solution.py:38
  90.2 0.8 collective-permute-start.18
  91.1 2.3 %collective-permute-done.19.refs_2_ = f32[16,256]{1,0:T(8,128)S(1)} collective-permute-done((f32[16,256]{1,0:T(8,128)S(1)}, f32[16,256]{1,0:T(8,128)S(1)}, u32[]{:S(2)}, u32[]{:S(2)}) %collective-permute-start.19) | collective-permute-done | bytes 16416 | tf_op jit(solution)/shard_map/ppermute | solution.py:38
  93.4 1.5 %collective-permute-done.18.refs_1_ = f32[16,256]{1,0:T(8,128)S(1)} collective-permute-done((f32[16,256]{1,0:T(8,128)S(1)}, f32[16,256]{1,0:T(8,128)S(1)}, u32[]{:S(2)}, u32[]{:S(2)}) %collective-permute-start.18) | collective-permute-done | bytes 16416 | tf_op jit(solution)/shard_map/ppermute | solution.py:38
  94.9 1.3 %shard_map.110 = (f32[1,128]{1,0:T(1,128)}, f32[1,128]{1,0:T(1,128)}) custom-call(f32[16,256]{1,0:T(8,128)S(1)} %shard_map.109.refs_0_, f32[16,256]{1,0:T(8,128)S(1)} %collective-permute-done.18.refs_1_, f32[16,256]{1,0:T(8,128)S(1)} %collective-permute-done.19.refs_2_, f32[16,256]{1,0:T(8,128)S(1)} %collective-permute-done.20.refs_3_), custom_call_target="tpu_custom_call" | custom-call | tf_op jit(solution)/shard_map/pallas_call | solution.py:279
  (34 shorter events, 0.6 us)
Async XLA Ops:
  3.5 17.0 %collective-permute-start = (bf16[64,4096]{1,0:T(8,128)(2,1)}, bf16[64,4096]{1,0:T(8,128)(2,1)S(1)}, u32[]{:S(2)}, u32[]{:S(2)}) collective-permute-start(bf16[64,4096]{1,0:T(8,128)(2,1)} %share.1.refs_2_), channel_id=1, source_target_pairs={{0,8},{1,9},{2,10},{3,11},{4,12},{5,13},{6,14},{7,15},{8,24},{9,25... | collective-permute-start | bytes 1572872 | tf_op jit(solution)/shard_map/ppermute | solution.py:38
  9.4 15.3 %collective-permute-start.4 = (bf16[64,4096]{1,0:T(8,128)(2,1)}, bf16[64,4096]{1,0:T(8,128)(2,1)S(1)}, u32[]{:S(2)}, u32[]{:S(2)}) collective-permute-start(bf16[64,4096]{1,0:T(8,128)(2,1)} %normalize.1.refs_3_), channel_id=1, source_target_pairs={{0,4},{1,5},{2,6},{3,7},{4,0},{5,1},{6,2},{7,3},{8,12},{9,13},{10,... | collective-permute-start | bytes 1572872 | tf_op jit(solution)/shard_map/ppermute | solution.py:38
  9.5 15.2 %collective-permute-start.3 = (bf16[64,4096]{1,0:T(8,128)(2,1)}, bf16[64,4096]{1,0:T(8,128)(2,1)S(1)}, u32[]{:S(2)}, u32[]{:S(2)}) collective-permute-start(bf16[64,4096]{1,0:T(8,128)(2,1)} %share.1.refs_2_), channel_id=1, source_target_pairs={{0,4},{1,5},{2,6},{3,7},{4,0},{5,1},{6,2},{7,3},{8,12},{9,13},{10,... | collective-permute-start | bytes 1572872 | tf_op jit(solution)/shard_map/ppermute | solution.py:38
  10.0 14.7 %copy-start = (bf16[64,4096]{1,0:T(8,128)(2,1)S(1)}, bf16[64,4096]{1,0:T(8,128)(2,1)}, u32[]{:S(2)}) copy-start(bf16[64,4096]{1,0:T(8,128)(2,1)} %share.1.refs_2_) | copy-start | bytes 1572868
  10.0 14.7 %copy-start.1 = (bf16[64,4096]{1,0:T(8,128)(2,1)S(1)}, bf16[64,4096]{1,0:T(8,128)(2,1)}, u32[]{:S(2)}) copy-start(bf16[64,4096]{1,0:T(8,128)(2,1)} %normalize.1.refs_3_) | copy-start | bytes 1572868
  10.0 14.7 %copy-start.2 = (s32[1024]{0:T(1024)S(1)}, s32[1024]{0:T(1024)}, u32[]{:S(2)}) copy-start(s32[1024]{0:T(1024)} %param.13) | copy-start | bytes 12292
  20.4 19.7 %collective-permute-start.7 = (bf16[64,4096]{1,0:T(8,128)(2,1)S(1)}, bf16[64,4096]{1,0:T(8,128)(2,1)S(1)}, u32[]{:S(2)}, u32[]{:S(2)}) collective-permute-start(bf16[64,4096]{1,0:T(8,128)(2,1)S(1)} %collective-permute-done.refs_3_), channel_id=1, source_target_pairs={{0,4},{1,5},{2,6},{3,7},{4,0},{5,1},{6,2},{7,3},{8,12},{9,13},{10,... | collective-permute-start | bytes 1572872 | tf_op jit(solution)/shard_map/ppermute | solution.py:38
  20.6 14.3 %collective-permute-start.2 = (bf16[64,4096]{1,0:T(8,128)(2,1)S(1)}, bf16[64,4096]{1,0:T(8,128)(2,1)S(1)}, u32[]{:S(2)}, u32[]{:S(2)}) collective-permute-start(bf16[64,4096]{1,0:T(8,128)(2,1)S(1)} %collective-permute-done.refs_3_), channel_id=1, source_target_pairs={{0,1},{1,0},{2,3},{3,2},{4,5},{5,4},{6,7},{7,6},{8,9},{9,8},{10,11... | collective-permute-start | bytes 1572872 | tf_op jit(solution)/shard_map/ppermute | solution.py:38
  22.1 14.9 %collective-permute-start.1 = (bf16[64,4096]{1,0:T(8,128)(2,1)S(1)}, bf16[64,4096]{1,0:T(8,128)(2,1)S(1)}, u32[]{:S(2)}, u32[]{:S(2)}) collective-permute-start(bf16[64,4096]{1,0:T(8,128)(2,1)S(1)} %collective-permute-done.refs_3_), channel_id=1, source_target_pairs={{0,8},{1,9},{2,10},{3,11},{4,12},{5,13},{6,14},{7,15},{8,24},{9,25... | collective-permute-start | bytes 1572872 | tf_op jit(solution)/shard_map/ppermute | solution.py:38
  34.8 5.3 %collective-permute-start.8 = (bf16[64,4096]{1,0:T(8,128)(2,1)S(1)}, bf16[64,4096]{1,0:T(8,128)(2,1)S(1)}, u32[]{:S(2)}, u32[]{:S(2)}) collective-permute-start(bf16[64,4096]{1,0:T(8,128)(2,1)S(1)} %collective-permute-done.2.refs_4_), channel_id=1, source_target_pairs={{0,4},{1,5},{2,6},{3,7},{4,0},{5,1},{6,2},{7,3},{8,12},{9,13},{10,... | collective-permute-start | bytes 1572872 | tf_op jit(solution)/shard_map/ppermute | solution.py:38
  37.0 17.0 %collective-permute-start.10 = (bf16[64,4096]{1,0:T(8,128)(2,1)S(1)}, bf16[64,4096]{1,0:T(8,128)(2,1)S(1)}, u32[]{:S(2)}, u32[]{:S(2)}) collective-permute-start(bf16[64,4096]{1,0:T(8,128)(2,1)S(1)} %collective-permute-done.1.refs_3_), channel_id=1, source_target_pairs={{0,4},{1,5},{2,6},{3,7},{4,0},{5,1},{6,2},{7,3},{8,12},{9,13},{10,... | collective-permute-start | bytes 1572872 | tf_op jit(solution)/shard_map/ppermute | solution.py:38
  37.0 14.3 %collective-permute-start.6 = (bf16[64,4096]{1,0:T(8,128)(2,1)S(1)}, bf16[64,4096]{1,0:T(8,128)(2,1)S(1)}, u32[]{:S(2)}, u32[]{:S(2)}) collective-permute-start(bf16[64,4096]{1,0:T(8,128)(2,1)S(1)} %collective-permute-done.1.refs_3_), channel_id=1, source_target_pairs={{0,2},{1,3},{2,0},{3,1},{4,6},{5,7},{6,4},{7,5},{8,10},{9,11},{10,... | collective-permute-start | bytes 1572872 | tf_op jit(solution)/shard_map/ppermute | solution.py:38
  38.5 15.0 %collective-permute-start.5 = (bf16[64,4096]{1,0:T(8,128)(2,1)S(1)}, bf16[64,4096]{1,0:T(8,128)(2,1)S(1)}, u32[]{:S(2)}, u32[]{:S(2)}) collective-permute-start(bf16[64,4096]{1,0:T(8,128)(2,1)S(1)} %collective-permute-done.1.refs_3_), channel_id=1, source_target_pairs={{0,8},{1,9},{2,10},{3,11},{4,12},{5,13},{6,14},{7,15},{8,24},{9,25... | collective-permute-start | bytes 1572872 | tf_op jit(solution)/shard_map/ppermute | solution.py:38
  49.9 35.6 %copy-start.3 = (f32[128]{0:T(128)S(1)}, f32[128]{0:T(128)}, u32[]{:S(2)}) copy-start(f32[128]{0:T(128)} %param.14) | copy-start | bytes 1540
  49.9 35.6 %copy-start.4 = (f32[128]{0:T(128)S(1)}, f32[128]{0:T(128)}, u32[]{:S(2)}) copy-start(f32[128]{0:T(128)} %param.15) | copy-start | bytes 1540
  49.9 35.6 %copy-start.5 = (f32[128]{0:T(128)S(1)}, f32[128]{0:T(128)}, u32[]{:S(2)}) copy-start(f32[128]{0:T(128)} %param.16) | copy-start | bytes 1540
  49.9 35.6 %copy-start.6 = (s32[128]{0:T(128)S(1)}, s32[128]{0:T(128)}, u32[]{:S(2)}) copy-start(s32[128]{0:T(128)} %param.17) | copy-start | bytes 1540
  51.3 2.7 %collective-permute-start.11 = (bf16[64,4096]{1,0:T(8,128)(2,1)S(1)}, bf16[64,4096]{1,0:T(8,128)(2,1)S(1)}, u32[]{:S(2)}, u32[]{:S(2)}) collective-permute-start(bf16[64,4096]{1,0:T(8,128)(2,1)S(1)} %collective-permute-done.6.refs_4_), channel_id=1, source_target_pairs={{0,4},{1,5},{2,6},{3,7},{4,0},{5,1},{6,2},{7,3},{8,12},{9,13},{10,... | collective-permute-start | bytes 1572872 | tf_op jit(solution)/shard_map/ppermute | solution.py:38
  53.4 14.3 %collective-permute-start.12 = (bf16[64,4096]{1,0:T(8,128)(2,1)S(1)}, bf16[64,4096]{1,0:T(8,128)(2,1)S(1)}, u32[]{:S(2)}, u32[]{:S(2)}) collective-permute-start(bf16[64,4096]{1,0:T(8,128)(2,1)S(1)} %collective-permute-done.5.refs_3_), channel_id=1, source_target_pairs={{0,4},{1,5},{2,6},{3,7},{4,0},{5,1},{6,2},{7,3},{8,12},{9,13},{10,... | collective-permute-start | bytes 1572872 | tf_op jit(solution)/shard_map/ppermute | solution.py:38
  53.4 14.3 %collective-permute-start.9 = (bf16[64,4096]{1,0:T(8,128)(2,1)S(1)}, bf16[64,4096]{1,0:T(8,128)(2,1)S(1)}, u32[]{:S(2)}, u32[]{:S(2)}) collective-permute-start(bf16[64,4096]{1,0:T(8,128)(2,1)S(1)} %collective-permute-done.5.refs_3_), channel_id=1, source_target_pairs={{0,1},{1,0},{2,3},{3,2},{4,5},{5,4},{6,7},{7,6},{8,9},{9,8},{10,11... | collective-permute-start | bytes 1572872 | tf_op jit(solution)/shard_map/ppermute | solution.py:38
  67.8 1.9 %collective-permute-start.13 = (bf16[64,4096]{1,0:T(8,128)(2,1)S(1)}, bf16[64,4096]{1,0:T(8,128)(2,1)S(1)}, u32[]{:S(2)}, u32[]{:S(2)}) collective-permute-start(bf16[64,4096]{1,0:T(8,128)(2,1)S(1)} %collective-permute-done.9.refs_4_), channel_id=1, source_target_pairs={{0,4},{1,5},{2,6},{3,7},{4,0},{5,1},{6,2},{7,3},{8,12},{9,13},{10,... | collective-permute-start | bytes 1572872 | tf_op jit(solution)/shard_map/ppermute | solution.py:38
  79.7 4.7 %collective-permute-start.16 = (f32[4,3,256]{2,1,0:T(4,128)S(1)}, f32[4,3,256]{2,1,0:T(4,128)S(1)}, u32[]{:S(2)}, u32[]{:S(2)}) collective-permute-start(f32[4,3,256]{2,1,0:T(4,128)S(1)} %shard_map.107.refs_0_), channel_id=1, source_target_pairs={{0,3},{1,2},{2,1},{3,0},{4,7},{5,6},{6,5},{7,4},{8,11},{9,10},{10,... | collective-permute-start | bytes 36872 | tf_op jit(solution)/shard_map/ppermute | solution.py:38
  80.2 4.2 %collective-permute-start.15 = (f32[4,3,256]{2,1,0:T(4,128)S(1)}, f32[4,3,256]{2,1,0:T(4,128)S(1)}, u32[]{:S(2)}, u32[]{:S(2)}) collective-permute-start(f32[4,3,256]{2,1,0:T(4,128)S(1)} %shard_map.107.refs_0_), channel_id=1, source_target_pairs={{0,2},{1,3},{2,0},{3,1},{4,6},{5,7},{6,4},{7,5},{8,10},{9,11},{10,... | collective-permute-start | bytes 36872 | tf_op jit(solution)/shard_map/ppermute | solution.py:38
  81.7 3.7 %collective-permute-start.14 = (f32[4,3,256]{2,1,0:T(4,128)S(1)}, f32[4,3,256]{2,1,0:T(4,128)S(1)}, u32[]{:S(2)}, u32[]{:S(2)}) collective-permute-start(f32[4,3,256]{2,1,0:T(4,128)S(1)} %shard_map.107.refs_0_), channel_id=1, source_target_pairs={{0,1},{1,0},{2,3},{3,2},{4,5},{5,4},{6,7},{7,6},{8,9},{9,8},{10,11... | collective-permute-start | bytes 36872 | tf_op jit(solution)/shard_map/ppermute | solution.py:38
  85.7 1.2 %collective-permute-start.17 = (f32[16,256]{1,0:T(8,128)S(1)}, f32[16,256]{1,0:T(8,128)S(1)}, u32[]{:S(2)}, u32[]{:S(2)}) collective-permute-start(f32[16,256]{1,0:T(8,128)S(1)} %shard_map.108.refs_0_), channel_id=1, source_target_pairs={{0,4},{1,5},{2,6},{3,7},{4,0},{5,1},{6,2},{7,3},{8,12},{9,13},{10,... | collective-permute-start | bytes 49160 | tf_op jit(solution)/shard_map/ppermute | solution.py:38
  87.0 4.0 %collective-permute-start.20 = (f32[16,256]{1,0:T(8,128)S(1)}, f32[16,256]{1,0:T(8,128)S(1)}, u32[]{:S(2)}, u32[]{:S(2)}) collective-permute-start(f32[16,256]{1,0:T(8,128)S(1)} %shard_map.109.refs_0_), channel_id=1, source_target_pairs={{0,16},{1,17},{2,18},{3,19},{4,20},{5,21},{6,22},{7,23},{8,0},{9,1... | collective-permute-start | bytes 49160 | tf_op jit(solution)/shard_map/ppermute | solution.py:38
  87.8 5.5 %collective-permute-start.19 = (f32[16,256]{1,0:T(8,128)S(1)}, f32[16,256]{1,0:T(8,128)S(1)}, u32[]{:S(2)}, u32[]{:S(2)}) collective-permute-start(f32[16,256]{1,0:T(8,128)S(1)} %shard_map.109.refs_0_), channel_id=1, source_target_pairs={{0,24},{1,25},{2,26},{3,27},{4,28},{5,29},{6,30},{7,31},{8,16},{9,... | collective-permute-start | bytes 49160 | tf_op jit(solution)/shard_map/ppermute | solution.py:38
  90.2 4.6 %collective-permute-start.18 = (f32[16,256]{1,0:T(8,128)S(1)}, f32[16,256]{1,0:T(8,128)S(1)}, u32[]{:S(2)}, u32[]{:S(2)}) collective-permute-start(f32[16,256]{1,0:T(8,128)S(1)} %shard_map.109.refs_0_), channel_id=1, source_target_pairs={{0,8},{1,9},{2,10},{3,11},{4,12},{5,13},{6,14},{7,15},{8,24},{9,25... | collective-permute-start | bytes 49160 | tf_op jit(solution)/shard_map/ppermute | solution.py:38
